TPU v7x, 32 devices: a whole 2x2x4 slice. The times are simulated.
32 devices in a mesh: row: 4 (over y, x), col: 8 (over z, core).
Axes of the slice: x: 2, y: 2, z: 4, core: 2. Of those that a mesh axis runs over, the one named last changes fastest.
Arguments:
- top_coeffs: float32 [8, 32768], P(None, ('row', 'col')), may hold values from -6 to 6
- fresh_one: bfloat16 [56, 32768], P(None, ('row', 'col')), may hold values from -6 to 6
- fresh_two: bfloat16 [56, 8, 32768], P(None, None, ('row', 'col')), may hold values from -6 to 6
- fresh_three: bfloat16 [56, 64, 32768], P(None, None, ('row', 'col')), may hold values from -6 to 6
- mixing: bfloat16 [64, 64], replicated, may hold values from -0.75 to 0.75
- transfer: float32 [1024, 1024], P(None, 'col'), may hold values from 0.1 to 1, as said below
Outputs:
- density: float32 [16, 1024, 1024], P('row', 'col')
Inputs may be any that keep to these rules, and one draw needn't show every extreme that they name: transfer is even: its value at the positions of modes (ky, kz) equals its value at the positions of modes (-ky mod 1024, -kz mod 1024).
All inputs are finite; a program needn't handle non-finite values.
Results may differ from a plain program's by a relative error of at most 0.0003.
Values sent between devices are 32-bit elements; how exact they have to be, the bound alone decides.
No kernel may reach another device: no remote copies, remote signals or barrier semaphores. Data moves between devices by JAX's collectives and lax.ppermute only.
A program may use at most 192 MiB of HBM per device.

v0:
```python
import functools
import math

import jax
import jax.numpy as jnp
import numpy as np
from jax import lax
from jax.experimental import pallas as pl
from jax.experimental.pallas import tpu as pltpu
from jax.sharding import PartitionSpec as P

F32 = jnp.float32
BF16 = jnp.bfloat16
LANES = 128
VMEM_LIMIT = 60 * 1024 * 1024


def bits_of(count):
    return count.bit_length() - 1


class Plan:
    def __init__(self, n_row, n_col, slots, grid):
        self.n_row, self.n_col, self.slots, self.grid = n_row, n_col, slots, grid
        self.owners = n_row * n_col
        self.planes = 16 // n_row
        self.pairs = self.planes // 2
        self.dest_x = n_row // 2
        self.blocks = grid // 8
        self.strip = self.blocks // n_col
        self.inner = slots // (2 * n_col)
        self.major = grid // LANES
        self.quarter = grid // 4
        own_bits = bits_of(self.owners)
        self.own_w = [k for k in range(own_bits) if k % 2 == 0]
        self.own_q = [k for k in range(own_bits) if k % 2 == 1]
        y_bits, z_bits = bits_of(self.strip), bits_of(self.blocks)
        code = []
        for k in range(y_bits):
            code += [("w", k), ("q", k)]
        code += [("w", k) for k in range(y_bits, z_bits)]
        self.inner_bits = code[own_bits:]
        top = bits_of(n_col)
        self.top_w = list(range(z_bits - top, z_bits))
        self.q_in = [k for kind, k in self.inner_bits if kind == "q"]
        self.mid_w = [k for kind, k in self.inner_bits if kind == "w" and k not in self.top_w]
        self.t_low = bits_of(LANES // self.inner)
        self.w_kept = 2 ** len(self.mid_w)
        self.rows_rw = 2 * self.w_kept
        self.small = 2 ** (self.t_low + len(self.q_in))
        assert self.small == 8 and n_col == self.major and slots // 2 == 4 * LANES
        self.src_rows = self.rows_rw * 2 * self.small
        self.q_stack = LANES // self.src_rows
        self.q_rest = 2 ** len(self.own_q) // self.q_stack
        self.w_extra = 2 ** len(self.own_w) // 8
        assert self.w_extra * self.w_kept == 2

    def send_table(self):
        lane = np.arange(LANES)
        low_t, inner = lane // self.inner, lane % self.inner
        top = np.zeros(LANES, np.int64)
        small = low_t.copy()
        kept = np.zeros(LANES, np.int64)
        q_value = np.zeros(LANES, np.int64)
        for place, (kind, k) in enumerate(self.inner_bits):
            bit = (inner >> place) & 1
            if kind == "q":
                q_value += bit << self.q_in.index(k)
            elif k in self.top_w:
                top += bit << self.top_w.index(k)
            else:
                kept += bit << self.mid_w.index(k)
        small = (low_t << len(self.q_in)) + q_value
        table = np.zeros((self.n_col, 2, self.w_kept, self.small, 2, LANES))
        for c in range(self.n_col):
            angle = 2 * np.pi * (c * top % self.n_col) / self.n_col
            cos, sin = np.cos(angle), np.sin(angle)
            table[c, 0, kept, small, 0, lane] = cos
            table[c, 0, kept, small, 1, lane] = sin
            table[c, 1, kept, small, 0, lane] = -sin
            table[c, 1, kept, small, 1, lane] = cos
        return table.reshape(self.n_col * self.rows_rw * self.small, 2 * LANES)

    def lane_z(self):
        lane = np.arange(LANES)
        return (lane >> 4) * 8 + ((lane >> 3) & 1) * 4 + (lane & 3), (lane >> 2) & 1

    def z_table(self):
        low, y_bit = self.lane_z()
        k = np.arange(LANES)
        table = np.zeros((2, 2, LANES, 2, 2, LANES))
        for kept in range(2):
            phase = np.outer(64 * kept + low, k) % LANES
            cos, sin = np.cos(2 * np.pi * phase / LANES), np.sin(2 * np.pi * phase / LANES)
            for b in range(2):
                mask = (y_bit == b)[:, None]
                table[kept, 0, :, b, 0] = cos * mask
                table[kept, 1, :, b, 0] = sin * mask
                table[kept, 0, :, b, 1] = -sin * mask
                table[kept, 1, :, b, 1] = cos * mask
        return table.reshape(4 * LANES, 4 * LANES)

    def y_rows(self):
        shape = (2, self.q_rest, 4, self.q_stack, self.small)
        y0, q_rest, y21, q_stack, small = np.indices(shape)
        n_in = len(self.q_in)
        t_low, q_in = small >> n_in, small & (2 ** n_in - 1)
        q_local = q_in * 2 ** len(self.own_q) + q_rest * self.q_stack + q_stack
        return (t_low * LANES + q_local * 8 + y21 * 2 + y0).reshape(-1)

    def m_rows(self):
        step = self.major // 4
        return (np.arange(step)[:, None] + step * np.arange(LANES)[None, :]).reshape(-1)

    def y_tables(self):
        n2, m, size = self.y_rows(), self.m_rows(), self.quarter
        angle = 2 * np.pi * (np.outer(m, n2) % size) / size
        cos, sin = np.cos(angle), np.sin(angle)
        ahead = np.block([[cos, sin], [-sin, cos]])
        angle = 2 * np.pi * (np.outer(np.arange(size), m) % size) / size
        cos, sin = np.cos(angle), np.sin(angle)
        return ahead, np.block([[cos, -sin], [sin, cos]])

    def turns(self):
        out = np.zeros((2, self.quarter, LANES), np.float32)
        for order, n2 in enumerate((self.y_rows(), np.arange(self.quarter))):
            for j in range(4):
                angle = 2 * np.pi * (n2 * j) / self.grid
                out[order, :, j] = np.cos(angle)
                out[order, :, 8 + j] = np.sin(angle)
        return out

    def z_back(self):
        n = np.arange(LANES)
        angle = 2 * np.pi * (np.outer(n, n) % LANES) / LANES
        cos, sin = np.cos(angle), np.sin(angle)
        return np.block([[cos, sin], [-sin, cos]])

    def src(self, w, q):
        index = 0
        for place, bit in enumerate(self.own_w):
            index |= ((w >> place) & 1) << bit
        for place, bit in enumerate(self.own_q):
            index |= ((q >> place) & 1) << bit
        return index


def halves(table):
    high = np.asarray(table, np.float32).astype(BF16)
    low = (np.asarray(table, np.float64) - high.astype(np.float64)).astype(BF16)
    return np.stack((high, low))


def split(x):
    high = x.astype(BF16)
    return high, (x - high.astype(F32)).astype(BF16)


def dot(a, b):
    return jnp.dot(a, b, preferred_element_type=F32)


def dot_nt(a, b):
    return lax.dot_general(a, b, (((1,), (1,)), ((), ())), preferred_element_type=F32)


def three(f, a, b):
    return f(a[0], b[0]) + (f(a[0], b[1]) + f(a[1], b[0]))


def one_hot(shape, hit):
    row = lax.broadcasted_iota(jnp.int32, shape, 0)
    col = lax.broadcasted_iota(jnp.int32, shape, 1)
    return jnp.where(hit(row, col), 1.0, 0.0).astype(BF16)


def spread(mixing, rows, row_of, same, fresh):
    pick = one_hot((rows, 64), lambda r, c: c == row_of(r))
    if fresh:
        wide = one_hot((64, 448), lambda r, c: r == 8 + c // 8)
        cell = lambda c: c % 8
    else:
        wide = one_hot((64, 64), lambda r, c: r == c % 8)
        cell = lambda c: c // 8
    table = dot(dot(pick, mixing).astype(BF16), wide)
    row = lax.broadcasted_iota(jnp.int32, table.shape, 0)
    col = lax.broadcasted_iota(jnp.int32, table.shape, 1)
    return jnp.where(same(row) == cell(col), table, 0.0).astype(BF16)


def carry(table, parents):
    high = parents.astype(BF16)
    rest = parents - high.astype(F32)
    mid = rest.astype(BF16)
    low = (rest - mid.astype(F32)).astype(BF16)
    return dot(table, high) + (dot(table, mid) + dot(table, low))


def expand_kernel(plan, top, one, two, three_ref, mixing, send, *refs):
    outs = refs[: plan.pairs]
    leaf, w2f, w2p, w3f, w3p = refs[plan.pairs :]

    @pl.when(pl.program_id(0) == 0)
    def _():
        mix = mixing[...]
        w2f[...] = spread(mix, 512, lambda r: r % 64, lambda r: r // 64, True)
        w2p[...] = spread(mix, 512, lambda r: r % 64, lambda r: r // 64, False)
        child = lambda r: 8 * (4 * (r // 32 % 2) + 2 * (r // 4 % 2) + r % 2)
        cell = lambda r: 4 * (r // 16 % 2) + 2 * (r // 8 % 2) + r // 2 % 2
        w3f[...] = spread(mix, 64, child, cell, True)
        w3p[...] = spread(mix, 64, child, cell, False)

    mix = mixing[...]
    level = carry(mix[:, :8], top[...]) + dot(mix[:, 8:], one[...])
    for g in range(8):
        rows = pl.ds(64 * g, 64)
        second = dot(w2f[rows, :], two[...]) + carry(w2p[rows, :], level)
        fresh = three_ref[:, pl.ds(8 * g, 8), :].reshape(448, second.shape[1])
        leaf[g] = dot(w3f[...], fresh) + carry(w3p[...], second)
    table = (send[0], send[1])
    for x in range(4):
        x2, x1 = x // 2, x % 2
        pair, dest = x % plan.pairs, x // plan.pairs
        for high in range(2):
            parts = []
            for part in range(2):
                pieces = [
                    leaf[4 * x2 + yz, pl.ds(32 * part + 16 * x1, 16), pl.ds((2 * high + tau) * LANES, LANES)]
                    for tau in range(2)
                    for yz in range(4)
                ]
                parts.append(jnp.concatenate(pieces, axis=0))
            data = split(jnp.concatenate(parts, axis=1))
            sent = three(dot_nt, table, data)
            outs[pair][0, dest, :, :, high] = sent.reshape(plan.n_col, plan.rows_rw, plan.small, LANES)


def expand(plan, top, one, two, three_in, mixing):
    half = plan.slots // 2
    shape = (2, plan.dest_x, plan.n_col, plan.rows_rw, 2, plan.small, LANES)
    table = halves(plan.send_table())
    whole = lambda array: pl.BlockSpec(array.shape, lambda i: (0,) * array.ndim)
    return pl.pallas_call(
        functools.partial(expand_kernel, plan),
        grid=(2,),
        in_specs=[
            pl.BlockSpec((8, half), lambda i: (0, i)),
            pl.BlockSpec((56, half), lambda i: (0, i)),
            pl.BlockSpec((448, half), lambda i: (0, i)),
            pl.BlockSpec((56, 64, half), lambda i: (0, 0, i)),
            whole(mixing),
            whole(table),
        ],
        out_specs=[pl.BlockSpec((1,) + shape[1:], lambda i: (i, 0, 0, 0, 0, 0, 0))] * plan.pairs,
        out_shape=[jax.ShapeDtypeStruct(shape, F32)] * plan.pairs,
        scratch_shapes=[
            pltpu.VMEM((8, 64, half), F32),
            pltpu.VMEM((512, 448), BF16),
            pltpu.VMEM((512, 64), BF16),
            pltpu.VMEM((64, 448), BF16),
            pltpu.VMEM((64, 64), BF16),
        ],
        compiler_params=pltpu.CompilerParams(vmem_limit_bytes=VMEM_LIMIT),
        name="expand",
    )(top, one, two.reshape(448, plan.slots), three_in, mixing, jnp.asarray(table))


def dft4(parts, sign):
    (ar, ai), (br, bi), (cr, ci), (dr, di) = parts
    pr, pi, mr, mi = ar + cr, ai + ci, ar - cr, ai - ci
    qr, qi, nr, ni = br + dr, bi + di, br - dr, bi - di
    return [
        (pr + qr, pi + qi),
        (mr - sign * ni, mi + sign * nr),
        (pr - qr, pi - qi),
        (mr + sign * ni, mi - sign * nr),
    ]


def middle_kernel(plan, got, factor, lane_turn, z_in, y_in, y_out, turns, z_out, out, flipped, prep):
    q_tiles = plan.q_rest * 4 * plan.q_stack
    for q_rest in range(plan.q_rest):
        for extra in range(plan.w_extra):
            for w in range(8):
                stack = [
                    got[plan.src(extra * 8 + w, q_rest * plan.q_stack + q)].reshape(plan.src_rows, LANES)
                    for q in range(plan.q_stack)
                ]
                flipped[w] = jnp.concatenate(stack, axis=0).T.reshape(16, 8, LANES)
            for tau in range(2):
                for y21 in range(4):
                    y2, y1 = y21 // 2, y21 % 2
                    pieces = [
                        flipped[w, 8 * tau + 4 * y2 + 2 * z2 + y1] for w in range(8) for z2 in range(2)
                    ]
                    block = jnp.concatenate(pieces, axis=0).T
                    block = block.reshape(plan.q_stack, 2, plan.w_kept, 2, 8, LANES)
                    for kept_in in range(plan.w_kept):
                        kept = extra if plan.w_extra == 2 else kept_in
                        cos = lane_turn[2 * kept : 2 * kept + 1, :]
                        sin = lane_turn[2 * kept + 1 : 2 * kept + 2, :]
                        for q in range(plan.q_stack):
                            for high in range(2):
                                re, im = block[q, 0, kept_in, high], block[q, 1, kept_in, high]
                                tile = (2 * high + tau) * q_tiles + (q_rest * 4 + y21) * plan.q_stack + q
                                rows = pl.ds(8 * tile, 8)
                                prep[rows, pl.ds(2 * kept * LANES, LANES)] = re * cos + im * sin
                                prep[rows, pl.ds((2 * kept + 1) * LANES, LANES)] = im * cos - re * sin
    z_done = three(dot, split(prep[...]), (z_in[0], z_in[1]))
    size = 8 * q_tiles
    parts = []
    for tile in range(4):
        rows = z_done[tile * size : (tile + 1) * size]
        column = lambda k: rows[:, k * LANES : (k + 1) * LANES]
        parts.append(
            (
                jnp.concatenate((column(0), column(2)), axis=0),
                jnp.concatenate((column(1), column(3)), axis=0),
            )
        )
    columns = []
    for j, (re, im) in enumerate(dft4(parts, -1.0)):
        if j:
            cos, sin = turns[0, :, j : j + 1], turns[0, :, 8 + j : 9 + j]
            re, im = re * cos + im * sin, im * cos - re * sin
        columns.append(jnp.concatenate((re, im), axis=0))
    ahead = three(dot, (y_in[0], y_in[1]), split(jnp.concatenate(columns, axis=1)))
    step = plan.major // 4
    scaled = []
    for j in range(4):
        own = ahead[:, j * LANES : (j + 1) * LANES]
        gain = jnp.concatenate([factor[pl.ds((j + 4 * m) * LANES, LANES), :] for m in range(step)], axis=0)
        scaled.append(own * jnp.concatenate((gain, gain), axis=0))
    back = three(dot, (y_out[0], y_out[1]), split(jnp.concatenate(scaled, axis=1)))
    parts = []
    for j in range(4):
        own = back[:, j * LANES : (j + 1) * LANES]
        re, im = own[: plan.quarter], own[plan.quarter :]
        if j:
            cos, sin = turns[1, :, j : j + 1], turns[1, :, 8 + j : 9 + j]
            re, im = re * cos - im * sin, im * cos + re * sin
        parts.append((re, im))
    lines = jnp.concatenate(
        [jnp.concatenate(part, axis=1) for part in dft4(parts, 1.0)], axis=0
    )
    done = three(dot, split(lines), (z_out[0], z_out[1]))
    cos, sin = lane_turn[4:5, :], lane_turn[5:6, :]
    re, im = done[:, :LANES], done[:, LANES:]
    out[:, 0] = (re * cos - im * sin).reshape(plan.n_col, LANES, LANES)
    out[:, 1] = (im * cos + re * sin).reshape(plan.n_col, LANES, LANES)


def middle(plan, got, factor, lane_turn, tables):
    return pl.pallas_call(
        functools.partial(middle_kernel, plan),
        out_shape=jax.ShapeDtypeStruct((plan.n_col, 2, LANES, LANES), F32),
        scratch_shapes=[
            pltpu.VMEM((8, 16, 8, LANES), F32),
            pltpu.VMEM((plan.grid // 2, 4 * LANES), F32),
        ],
        compiler_params=pltpu.CompilerParams(vmem_limit_bytes=VMEM_LIMIT),
        name="middle",
    )(got, factor, lane_turn, *tables)


def dft(parts, sign):
    size = len(parts)
    if size == 1:
        return parts
    even, odd = dft(parts[0::2], sign), dft(parts[1::2], sign)
    first, second = [], []
    for k in range(size // 2):
        (er, ei), (xr, xi) = even[k], odd[k]
        angle = 2 * math.pi * k / size
        if 4 * k == size:
            xr, xi = -sign * xi, sign * xr
        elif k:
            cos, sin = math.cos(angle), sign * math.sin(angle)
            xr, xi = xr * cos - xi * sin, xr * sin + xi * cos
        first.append((er + xr, ei + xi))
        second.append((er - xr, ei - xi))
    return first + second


def final_kernel(plan, got, *refs):
    out = refs[-1]
    scale = 1.0 / (plan.grid * plan.grid)
    step = 16

    @pl.loop(0, LANES // step)
    def _(i):
        rows = pl.ds(pl.multiple_of(i * step, step), step)
        parts = [(got[c, 0, rows, :], got[c, 1, rows, :]) for c in range(plan.n_col)]
        for w, (re, im) in enumerate(dft(parts, 1.0)):
            out[0, rows, pl.ds(w * LANES, LANES)] = re * scale
            out[1, rows, pl.ds(w * LANES, LANES)] = im * scale


def final(plan, pair, got, so_far):
    extra = [] if so_far is None else [so_far]
    shape = (plan.planes, LANES, plan.grid)
    return pl.pallas_call(
        functools.partial(final_kernel, plan),
        grid=(1,),
        in_specs=[pl.BlockSpec(got.shape, lambda i: (0, 0, 0, 0))]
        + [pl.BlockSpec(memory_space=pl.ANY) for _ in extra],
        out_specs=pl.BlockSpec((2, LANES, plan.grid), lambda i: (pair, 0, 0)),
        out_shape=jax.ShapeDtypeStruct(shape, F32),
        input_output_aliases={1: 0} if extra else {},
        compiler_params=pltpu.CompilerParams(vmem_limit_bytes=VMEM_LIMIT),
        name="final",
    )(got, *extra)


def lane_turns(plan):
    place, _ = plan.lane_z()
    low = np.stack((place, place + 64, np.arange(LANES))).astype(np.int32)
    phase = lax.axis_index("col") * jnp.asarray(low) % plan.grid
    angle = phase.astype(F32) * (2.0 * math.pi / plan.grid)
    both = jnp.stack((jnp.cos(angle), jnp.sin(angle)), axis=1).reshape(6, LANES)
    return jnp.concatenate((both, jnp.zeros((2, LANES), F32)), axis=0)


def body(n_row, n_col, top_coeffs, fresh_one, fresh_two, fresh_three, mixing, transfer):
    plan = Plan(n_row, n_col, top_coeffs.shape[1], transfer.shape[0])
    sends = expand(plan, top_coeffs, fresh_one, fresh_two, fresh_three, mixing)
    lane_turn = lane_turns(plan)
    y_in, y_out = plan.y_tables()
    tables = [
        jnp.asarray(t)
        for t in (halves(plan.z_table()), halves(y_in), halves(y_out), plan.turns(), halves(plan.z_back()))
    ]
    got = [
        lax.all_to_all(
            s.reshape(plan.owners, plan.src_rows, LANES), ("row", "col"), split_axis=0, concat_axis=0, tiled=True
        )
        for s in sends
    ]
    result = None
    for pair in range(plan.pairs):
        mid = middle(plan, got[pair], transfer, lane_turn, tables)
        back = lax.all_to_all(mid, "col", split_axis=0, concat_axis=0, tiled=True)
        result = final(plan, pair, back, result)
    return result


def solution(mesh):
    n_row, n_col = mesh.shape["row"], mesh.shape["col"]
    return jax.shard_map(
        functools.partial(body, n_row, n_col),
        mesh=mesh,
        in_specs=(
            P(None, ("row", "col")),
            P(None, ("row", "col")),
            P(None, None, ("row", "col")),
            P(None, None, ("row", "col")),
            P(),
            P(None, "col"),
        ),
        out_specs=P("row", "col", None),
        check_vma=False,
    )
```

profile of v0, /device:TPU:0, one launch (start us, length us, event | category | flops | bytes accessed | tf_op | source)
XLA Modules:
  0.0 141.1 jit_solution(6786513245944722964)
XLA Ops:
  0.0 12.6 %expand.1 = (f32[2,2,8,4,2,8,128]{6,5,4,3,2,1,0:T(8,128)}, f32[2,2,8,4,2,8,128]{6,5,4,3,2,1,0:T(8,128)}) custom-call(f32[8,1024]{1,0:T(8,128)} %top.1, bf16[56,1024]{1,0:T(8,128)(2,1)} %one.1, bf16[448,1024]{1,0:T(8,128)(2,1)} %bitcast.6, bf16[56,64,1024]{2,1,0:T(8,128)(2,1)} %three_ref.1, bf16[64,64]{1,0:T(8,128)(2,1)} %mixing.1, ...), custom_call_target="tpu_custom_call" | custom-call | tf_op jit(solution)/shard_map/expand/pallas_call | solution.py:243
  12.6 0.0 copy-start.3
  12.6 34.9 %all_to_all.20.got = f32[32,64,128]{2,1,0:T(8,128)} all-to-all(f32[32,64,128]{2,1,0:T(8,128)} %bitcast.5), channel_id=1, replica_groups=mesh['row'=4,'col'=8] {'row','col'}, dimensions={0} | all-to-all | bytes 2097152 | tf_op jit(solution)/shard_map/all_to_all | solution.py:434
  47.5 2.6 %all-to-all-start = ((f32[32,64,128]{2,1,0:T(8,128)}), f32[32,64,128]{2,1,0:T(8,128)S(1)}, u32[]{:S(2)}, u32[]{:S(2)}) async-start(f32[32,64,128]{2,1,0:T(8,128)} %bitcast.1), calls=%async_computation | async-start | bytes 2097152 | tf_op jit(solution)/shard_map/all_to_all | solution.py:434
  50.2 0.0 copy-done.3
  50.2 0.1 cosine_bitcast_fusion
  50.3 0.6 concatenate.3.lane_turn
  50.9 7.8 %middle.3 = f32[8,2,128,128]{3,2,1,0:T(8,128)} custom-call(f32[32,64,128]{2,1,0:T(8,128)} %all_to_all.20.got, f32[1024,128]{1,0:T(8,128)} %factor.3, f32[8,128]{1,0:T(8,128)} %concatenate.3.lane_turn, bf16[2,512,512]{2,1,0:T(8,128)(2,1)} %constant.39.clone.z_in, bf16[2,512,512]{2,1,0:T(8,128)(2,1)} %constant.40.clone.y_in, ...), custom_call_target="tpu_custom_call" | custom-call | tf_op jit(solution)/shard_map/middle/pallas_call | solution.py:354
  58.7 19.0 %all-to-all-done.got = f32[32,64,128]{2,1,0:T(8,128)S(1)} async-done(((f32[32,64,128]{2,1,0:T(8,128)}), f32[32,64,128]{2,1,0:T(8,128)S(1)}, u32[]{:S(2)}, u32[]{:S(2)}) %all-to-all-start) | async-done | bytes 1048608 | tf_op jit(solution)/shard_map/all_to_all | solution.py:434
  77.6 0.0 copy-start.2
  77.6 3.6 %all-to-all-start.3 = ((f32[8,2,128,128]{3,2,1,0:T(8,128)}), f32[8,2,128,128]{3,2,1,0:T(8,128)S(1)}, u32[]{:S(2)}, u32[]{:S(2)}) async-start(f32[8,2,128,128]{3,2,1,0:T(8,128)} %middle.3), calls=%async_computation.3 | async-start | bytes 2097152 | tf_op jit(solution)/shard_map/all_to_all | solution.py:442
  81.2 0.0 copy-done.2
  81.2 7.8 %middle.2 = f32[8,2,128,128]{3,2,1,0:T(8,128)} custom-call(f32[32,64,128]{2,1,0:T(8,128)} %copy-done.2, f32[1024,128]{1,0:T(8,128)} %factor.3, f32[8,128]{1,0:T(8,128)} %concatenate.3.lane_turn, bf16[2,512,512]{2,1,0:T(8,128)(2,1)} %constant.39.clone.z_in, bf16[2,512,512]{2,1,0:T(8,128)(2,1)} %constant.40.clone.y_in, ...), custom_call_target="tpu_custom_call" | custom-call | tf_op jit(solution)/shard_map/middle/pallas_call | solution.py:354
  89.0 18.7 %all-to-all-done.3.got = f32[8,2,128,128]{3,2,1,0:T(8,128)S(1)} async-done(((f32[8,2,128,128]{3,2,1,0:T(8,128)}), f32[8,2,128,128]{3,2,1,0:T(8,128)S(1)}, u32[]{:S(2)}, u32[]{:S(2)}) %all-to-all-start.3) | async-done | bytes 1048608 | tf_op jit(solution)/shard_map/all_to_all | solution.py:442
  107.7 0.0 copy-start
  107.7 3.6 %all-to-all-start.1 = ((f32[8,2,128,128]{3,2,1,0:T(8,128)}), f32[8,2,128,128]{3,2,1,0:T(8,128)S(1)}, u32[]{:S(2)}, u32[]{:S(2)}) async-start(f32[8,2,128,128]{3,2,1,0:T(8,128)} %middle.2), calls=%async_computation.1 | async-start | bytes 2097152 | tf_op jit(solution)/shard_map/all_to_all | solution.py:442
  111.2 0.0 copy-done
  111.3 2.4 %final.2.refs_0_ = f32[4,128,1024]{2,1,0:T(8,128)} custom-call(f32[8,2,128,128]{3,2,1,0:T(8,128)} %copy-done), custom_call_target="tpu_custom_call" | custom-call | tf_op jit(solution)/shard_map/final/pallas_call | solution.py:402
  113.7 24.1 %all-to-all-done.1.got = f32[8,2,128,128]{3,2,1,0:T(8,128)S(1)} async-done(((f32[8,2,128,128]{3,2,1,0:T(8,128)}), f32[8,2,128,128]{3,2,1,0:T(8,128)S(1)}, u32[]{:S(2)}, u32[]{:S(2)}) %all-to-all-start.1) | async-done | bytes 1048608 | tf_op jit(solution)/shard_map/all_to_all | solution.py:442
  137.7 0.0 copy-start.1
  137.7 1.0 copy-done.1
  138.7 2.4 %final.3 = f32[4,128,1024]{2,1,0:T(8,128)} custom-call(f32[8,2,128,128]{3,2,1,0:T(8,128)} %copy-done.1, f32[4,128,1024]{2,1,0:T(8,128)} %final.2.refs_0_), custom_call_target="tpu_custom_call", output_to_operand_aliasing={{}: (1, {})} | custom-call | tf_op jit(solution)/shard_map/final/pallas_call | solution.py:402
  (4 shorter events, 0.0 us)
Async XLA Ops:
  12.6 37.6 %copy-start.3 = (s32[3,128]{1,0:T(4,128)S(1)}, s32[3,128]{1,0:T(4,128)}, u32[]{:S(2)}) copy-start(s32[3,128]{1,0:T(4,128)} %constant.38.clone) | copy-start | bytes 4612
  47.5 30.1 %all-to-all-start = ((f32[32,64,128]{2,1,0:T(8,128)}), f32[32,64,128]{2,1,0:T(8,128)S(1)}, u32[]{:S(2)}, u32[]{:S(2)}) async-start(f32[32,64,128]{2,1,0:T(8,128)} %bitcast.1), calls=%async_computation | async-start | bytes 2097152 | tf_op jit(solution)/shard_map/all_to_all | solution.py:434
  77.6 3.6 %copy-start.2 = (f32[32,64,128]{2,1,0:T(8,128)}, f32[32,64,128]{2,1,0:T(8,128)S(1)}, u32[]{:S(2)}) copy-start(f32[32,64,128]{2,1,0:T(8,128)S(1)} %all-to-all-done.got) | copy-start | bytes 3145732
  77.6 30.1 %all-to-all-start.3 = ((f32[8,2,128,128]{3,2,1,0:T(8,128)}), f32[8,2,128,128]{3,2,1,0:T(8,128)S(1)}, u32[]{:S(2)}, u32[]{:S(2)}) async-start(f32[8,2,128,128]{3,2,1,0:T(8,128)} %middle.3), calls=%async_computation.3 | async-start | bytes 2097152 | tf_op jit(solution)/shard_map/all_to_all | solution.py:442
  107.7 3.6 %copy-start = (f32[8,2,128,128]{3,2,1,0:T(8,128)}, f32[8,2,128,128]{3,2,1,0:T(8,128)S(1)}, u32[]{:S(2)}) copy-start(f32[8,2,128,128]{3,2,1,0:T(8,128)S(1)} %all-to-all-done.3.got) | copy-start | bytes 3145732
  107.7 30.1 %all-to-all-start.1 = ((f32[8,2,128,128]{3,2,1,0:T(8,128)}), f32[8,2,128,128]{3,2,1,0:T(8,128)S(1)}, u32[]{:S(2)}, u32[]{:S(2)}) async-start(f32[8,2,128,128]{3,2,1,0:T(8,128)} %middle.2), calls=%async_computation.1 | async-start | bytes 2097152 | tf_op jit(solution)/shard_map/all_to_all | solution.py:442
  137.7 1.0 copy-start.1
where the time goes:
time: 142 us; the launch traced here: 141 us
  waiting for transfers between devices  61.8 us (44%)
  blocking collectives  34.9 us (25%)
  Pallas kernels  33 us (23%)
  starting transfers between devices  9.76 us (7%)
  local copies, waits for them, and re-layouts  1.6 us (1%)
    all_to_all x2, waiting for transfers between devices, body(): back = lax.all_to_all(mid, 'col', split_axis=0, concat_axis=0, tiled=True)  42.8 us
    all_to_all x1, blocking collectives, body(): lax.all_to_all(s.reshape(plan.owners, plan.src_rows, LANES), ('row', 'col...  34.9 us
    all_to_all x1, waiting for transfers between devices, body(): lax.all_to_all(s.reshape(plan.owners, plan.src_rows, LANES), ('row', 'col...  19 us
    pallas_call x2, Pallas kernels, middle(): pl.pallas_call(functools.partial(middle_kernel, plan), out_shape=jax.Shap...  15.5 us
    pallas_call x1, Pallas kernels, expand(): pl.pallas_call(functools.partial(expand_kernel, plan), grid=(2,), in_spec...  12.6 us
    all_to_all x2, starting transfers between devices, body(): back = lax.all_to_all(mid, 'col', split_axis=0, concat_axis=0, tiled=True)  7.11 us
    pallas_call x2, Pallas kernels, final(): pl.pallas_call(functools.partial(final_kernel, plan), grid=(1,), in_specs...  4.82 us
  transfers between devices with their start and end apart: 3, of which 3 were waited for; matrix products, arithmetic and copies ran while one was open for 0% of the time, Pallas kernels for 13%

commit v1 on v0

--- a/solution.py
+++ b/solution.py
@@ -8,6 +8,7 @@
 from jax.experimental import pallas as pl
 from jax.experimental.pallas import tpu as pltpu
 from jax.sharding import PartitionSpec as P
+
 
 F32 = jnp.float32
 BF16 = jnp.bfloat16
@@ -54,6 +55,7 @@
         self.q_rest = 2 ** len(self.own_q) // self.q_stack
         self.w_extra = 2 ** len(self.own_w) // 8
         assert self.w_extra * self.w_kept == 2
+        assert self.pairs in (1, 2)
 
     def send_table(self):
         lane = np.arange(LANES)
@@ -197,10 +199,12 @@
 
 
 def expand_kernel(plan, top, one, two, three_ref, mixing, send, *refs):
-    outs = refs[: plan.pairs]
-    leaf, w2f, w2p, w3f, w3p = refs[plan.pairs :]
-
-    @pl.when(pl.program_id(0) == 0)
+    count = plan.pairs if plan.pairs == 1 else plan.n_row + 1
+    outs = refs[:count]
+    leaf, w2f, w2p, w3f, w3p, joined = refs[count:]
+    step = pl.program_id(0)
+
+    @pl.when(step == 0)
     def _():
         mix = mixing[...]
         w2f[...] = spread(mix, 512, lambda r: r % 64, lambda r: r // 64, True)
@@ -232,12 +236,30 @@
                 parts.append(jnp.concatenate(pieces, axis=0))
             data = split(jnp.concatenate(parts, axis=1))
             sent = three(dot_nt, table, data)
-            outs[pair][0, dest, :, :, high] = sent.reshape(plan.n_col, plan.rows_rw, plan.small, LANES)
+            sent = sent.reshape(plan.n_col, plan.rows_rw, plan.small, LANES)
+            if pair == 0:
+                outs[0][0, dest, :, :, high] = sent
+            else:
+                joined[step * plan.dest_x + dest, :, :, high] = sent
+
+    if plan.pairs > 1:
+
+        @pl.when(step == 1)
+        def _():
+            row, col = lax.axis_index("row"), lax.axis_index("col")
+            for far in range(plan.n_row):
+                for shift in range(plan.n_col):
+                    outs[1 + far][shift] = joined[row ^ far, col ^ shift]
 
 
 def expand(plan, top, one, two, three_in, mixing):
     half = plan.slots // 2
-    shape = (2, plan.dest_x, plan.n_col, plan.rows_rw, 2, plan.small, LANES)
+    block = (plan.n_col, plan.rows_rw, 2, plan.small, LANES)
+    shapes = [(2, plan.dest_x) + block]
+    specs = [pl.BlockSpec((1, plan.dest_x) + block, lambda i: (i, 0, 0, 0, 0, 0, 0))]
+    if plan.pairs > 1:
+        shapes += [block] * plan.n_row
+        specs += [pl.BlockSpec(block, lambda i: (0, 0, 0, 0, 0))] * plan.n_row
     table = halves(plan.send_table())
     whole = lambda array: pl.BlockSpec(array.shape, lambda i: (0,) * array.ndim)
     return pl.pallas_call(
@@ -251,14 +273,15 @@
             whole(mixing),
             whole(table),
         ],
-        out_specs=[pl.BlockSpec((1,) + shape[1:], lambda i: (i, 0, 0, 0, 0, 0, 0))] * plan.pairs,
-        out_shape=[jax.ShapeDtypeStruct(shape, F32)] * plan.pairs,
+        out_specs=specs,
+        out_shape=[jax.ShapeDtypeStruct(shape, F32) for shape in shapes],
         scratch_shapes=[
             pltpu.VMEM((8, 64, half), F32),
             pltpu.VMEM((512, 448), BF16),
             pltpu.VMEM((512, 64), BF16),
             pltpu.VMEM((64, 448), BF16),
             pltpu.VMEM((64, 64), BF16),
+            pltpu.VMEM((plan.n_row,) + block, F32),
         ],
         compiler_params=pltpu.CompilerParams(vmem_limit_bytes=VMEM_LIMIT),
         name="expand",
@@ -277,13 +300,24 @@
     ]
 
 
-def middle_kernel(plan, got, factor, lane_turn, z_in, y_in, y_out, turns, z_out, out, flipped, prep):
+def middle_kernel(plan, count, *refs):
+    parts, refs = refs[:count], refs[count:]
+    factor, lane_turn, z_in, y_in, y_out, turns, z_out = refs[:7]
+    outs = refs[7 : 7 + plan.n_col]
+    got, flipped, prep, out = refs[7 + plan.n_col :]
+    row, col = lax.axis_index("row"), lax.axis_index("col")
+    if count == 1:
+        got = parts[0]
+    else:
+        for shift in range(plan.n_col):
+            for far in range(plan.n_row):
+                got[(row ^ far) * plan.n_col + (col ^ shift)] = parts[shift][far]
     q_tiles = plan.q_rest * 4 * plan.q_stack
     for q_rest in range(plan.q_rest):
         for extra in range(plan.w_extra):
             for w in range(8):
                 stack = [
-                    got[plan.src(extra * 8 + w, q_rest * plan.q_stack + q)].reshape(plan.src_rows, LANES)
+                    got[plan.src(extra * 8 + w, q_rest * plan.q_stack + q)]
                     for q in range(plan.q_stack)
                 ]
                 flipped[w] = jnp.concatenate(stack, axis=0).T.reshape(16, 8, LANES)
@@ -348,19 +382,47 @@
     re, im = done[:, :LANES], done[:, LANES:]
     out[:, 0] = (re * cos - im * sin).reshape(plan.n_col, LANES, LANES)
     out[:, 1] = (im * cos + re * sin).reshape(plan.n_col, LANES, LANES)
-
-
-def middle(plan, got, factor, lane_turn, tables):
+    for shift in range(plan.n_col):
+        outs[shift][...] = out[col ^ shift]
+
+
+def middle(plan, parts, factor, lane_turn, tables):
     return pl.pallas_call(
-        functools.partial(middle_kernel, plan),
-        out_shape=jax.ShapeDtypeStruct((plan.n_col, 2, LANES, LANES), F32),
+        functools.partial(middle_kernel, plan, len(parts)),
+        out_shape=[jax.ShapeDtypeStruct((2, LANES, LANES), F32)] * plan.n_col,
         scratch_shapes=[
+            pltpu.VMEM((plan.owners, plan.src_rows, LANES), F32),
             pltpu.VMEM((8, 16, 8, LANES), F32),
             pltpu.VMEM((plan.grid // 2, 4 * LANES), F32),
+            pltpu.VMEM((plan.n_col, 2, LANES, LANES), F32),
         ],
         compiler_params=pltpu.CompilerParams(vmem_limit_bytes=VMEM_LIMIT),
         name="middle",
-    )(got, factor, lane_turn, *tables)
+    )(*parts, factor, lane_turn, *tables)
+
+
+def regroup_kernel(plan, *refs):
+    parts, outs = refs[: plan.n_row], refs[plan.n_row :]
+    for shift in range(plan.n_col):
+        for far in range(plan.n_row):
+            outs[shift][far] = parts[far][shift]
+
+
+def regroup(plan, parts):
+    return pl.pallas_call(
+        functools.partial(regroup_kernel, plan),
+        out_shape=[jax.ShapeDtypeStruct((plan.n_row, plan.src_rows, LANES), F32)] * plan.n_col,
+        compiler_params=pltpu.CompilerParams(vmem_limit_bytes=VMEM_LIMIT),
+        name="regroup",
+    )(*parts)
+
+
+def swap(parts, axis):
+    size = len(parts)
+    out = [parts[0]] + [None] * (size - 1)
+    for shift in reversed(range(1, size)):
+        out[shift] = lax.ppermute(parts[shift], axis, [(k, k ^ shift) for k in range(size)])
+    return out
 
 
 def dft(parts, sign):
@@ -382,10 +444,13 @@
     return first + second
 
 
-def final_kernel(plan, got, *refs):
-    out = refs[-1]
+def final_kernel(plan, *refs):
+    parts, out, got = refs[: plan.n_col], refs[-2], refs[-1]
     scale = 1.0 / (plan.grid * plan.grid)
     step = 16
+    col = lax.axis_index("col")
+    for shift in range(plan.n_col):
+        got[col ^ shift] = parts[shift][...]
 
     @pl.loop(0, LANES // step)
     def _(i):
@@ -396,20 +461,21 @@
             out[1, rows, pl.ds(w * LANES, LANES)] = im * scale
 
 
-def final(plan, pair, got, so_far):
+def final(plan, pair, parts, so_far):
     extra = [] if so_far is None else [so_far]
     shape = (plan.planes, LANES, plan.grid)
     return pl.pallas_call(
         functools.partial(final_kernel, plan),
         grid=(1,),
-        in_specs=[pl.BlockSpec(got.shape, lambda i: (0, 0, 0, 0))]
+        in_specs=[pl.BlockSpec((2, LANES, LANES), lambda i: (0, 0, 0))] * plan.n_col
         + [pl.BlockSpec(memory_space=pl.ANY) for _ in extra],
         out_specs=pl.BlockSpec((2, LANES, plan.grid), lambda i: (pair, 0, 0)),
         out_shape=jax.ShapeDtypeStruct(shape, F32),
-        input_output_aliases={1: 0} if extra else {},
+        scratch_shapes=[pltpu.VMEM((plan.n_col, 2, LANES, LANES), F32)],
+        input_output_aliases={plan.n_col: 0} if extra else {},
         compiler_params=pltpu.CompilerParams(vmem_limit_bytes=VMEM_LIMIT),
         name="final",
-    )(got, *extra)
+    )(*parts, *extra)
 
 
 def lane_turns(plan):
@@ -421,25 +487,26 @@
     return jnp.concatenate((both, jnp.zeros((2, LANES), F32)), axis=0)
 
 
-def body(n_row, n_col, top_coeffs, fresh_one, fresh_two, fresh_three, mixing, transfer):
+def steps(n_row, n_col, top_coeffs, fresh_one, fresh_two, fresh_three, mixing, transfer):
     plan = Plan(n_row, n_col, top_coeffs.shape[1], transfer.shape[0])
-    sends = expand(plan, top_coeffs, fresh_one, fresh_two, fresh_three, mixing)
+    sends = list(expand(plan, top_coeffs, fresh_one, fresh_two, fresh_three, mixing))
     lane_turn = lane_turns(plan)
     y_in, y_out = plan.y_tables()
     tables = [
         jnp.asarray(t)
         for t in (halves(plan.z_table()), halves(y_in), halves(y_out), plan.turns(), halves(plan.z_back()))
     ]
-    got = [
-        lax.all_to_all(
-            s.reshape(plan.owners, plan.src_rows, LANES), ("row", "col"), split_axis=0, concat_axis=0, tiled=True
-        )
-        for s in sends
-    ]
+    got = []
+    sent = sends[0].reshape(plan.owners, plan.src_rows, LANES)
+    got.append([lax.all_to_all(sent, ("row", "col"), split_axis=0, concat_axis=0, tiled=True)])
+    if plan.pairs > 1:
+        rows = swap([s.reshape(plan.n_col, plan.src_rows, LANES) for s in sends[1:]], "row")
+        columns = regroup(plan, rows)
+        got.append(swap(columns, "col"))
     result = None
     for pair in range(plan.pairs):
         mid = middle(plan, got[pair], transfer, lane_turn, tables)
-        back = lax.all_to_all(mid, "col", split_axis=0, concat_axis=0, tiled=True)
+        back = swap(mid, "col")
         result = final(plan, pair, back, result)
     return result
 
@@ -447,7 +514,7 @@
 def solution(mesh):
     n_row, n_col = mesh.shape["row"], mesh.shape["col"]
     return jax.shard_map(
-        functools.partial(body, n_row, n_col),
+        functools.partial(steps, n_row, n_col),
         mesh=mesh,
         in_specs=(
             P(None, ("row", "col")),

time: 142 us -> 149 us (1.049)
  the two profiles are of different devices: /device:TPU:0 before, /device:TPU:17 now
where the time goes in v1:
time: 149 us
  waiting for transfers between devices  72.5 us (49%)
  Pallas kernels  36.2 us (24%)
  starting transfers between devices  35.4 us (24%)
  local copies, waits for them, and re-layouts  4.19 us (3%)
    ppermute x24, waiting for transfers between devices, swap(): lax.ppermute(parts[shift], axis, [(k, k ^ shift) for k in range(size)])  72.5 us
    ppermute x24, starting transfers between devices, swap(): lax.ppermute(parts[shift], axis, [(k, k ^ shift) for k in range(size)])  29.2 us
    pallas_call x2, Pallas kernels, middle(): pl.pallas_call(functools.partial(middle_kernel, plan, len(parts)), out_sh...  15.8 us
    pallas_call x1, Pallas kernels, expand(): pl.pallas_call(functools.partial(expand_kernel, plan), grid=(2,), in_spec...  13 us
    all_to_all x1, starting transfers between devices, steps(): lax.all_to_all(sent, ('row', 'col'), split_axis=0, concat_axis=0, tiled=T...  6.24 us
    pallas_call x2, Pallas kernels, final(): pl.pallas_call(functools.partial(final_kernel, plan), grid=(1,), in_specs...  5.12 us
    unnamed x68, local copies, waits for them, and re-layouts  3.58 us
  transfers between devices with their start and end apart: 25, of which 14 were waited for; matrix products, arithmetic and copies ran while one was open for 0% of the time, Pallas kernels for 14%

profile of v1, /device:TPU:17, one launch (start us, length us, event | category | flops | bytes accessed | tf_op | source)
XLA Modules:
  0.0 148.7 jit_solution(7747221025600345105)
XLA Ops:
  0.0 13.0 %expand.1 = (f32[2,2,8,4,2,8,128]{6,5,4,3,2,1,0:T(8,128)}, f32[8,4,2,8,128]{4,3,2,1,0:T(8,128)}, f32[8,4,2,8,128]{4,3,2,1,0:T(8,128)}, f32[8,4,2,8,128]{4,3,2,1,0:T(8,128)}, f32[8,4,2,8,128]{4,3,2,1,0:T(8,128)}) custom-call(f32[8,1024]{1,0:T(8,128)} %top.1, bf16[56,1024]{1,0:T(8,128)(2,1)} %one.1, bf16[448,1024]{1,0:T(8,128)(2,1)} %bitcast.9, ...), custom_call_target="tpu_custom_call" | custom-call | tf_op jit(solution)/shard_map/expand/pallas_call | solution.py:265
  13.1 6.2 %all-to-all-start = ((f32[32,64,128]{2,1,0:T(8,128)}), f32[32,64,128]{2,1,0:T(8,128)S(1)}, u32[]{:S(2)}, u32[]{:S(2)}) async-start(f32[32,64,128]{2,1,0:T(8,128)} %bitcast.8), calls=%async_computation | async-start | bytes 2097152 | tf_op jit(solution)/shard_map/all_to_all | solution.py:501
  19.3 1.3 collective-permute-start
  20.6 1.2 collective-permute-start.1
  21.8 0.2 collective-permute-start.2
  22.1 13.7 %collective-permute-done.refs_1_ = f32[8,64,128]{2,1,0:T(8,128)S(1)} collective-permute-done((f32[8,64,128]{2,1,0:T(8,128)S(1)}, f32[8,64,128]{2,1,0:T(8,128)S(1)}, u32[]{:S(2)}, u32[]{:S(2)}) %collective-permute-start) | collective-permute-done | bytes 262176 | tf_op jit(solution)/shard_map/ppermute | solution.py:424
  35.8 9.3 %collective-permute-done.2.refs_3_ = f32[8,64,128]{2,1,0:T(8,128)S(1)} collective-permute-done((f32[8,64,128]{2,1,0:T(8,128)S(1)}, f32[8,64,128]{2,1,0:T(8,128)S(1)}, u32[]{:S(2)}, u32[]{:S(2)}) %collective-permute-start.2) | collective-permute-done | bytes 262176 | tf_op jit(solution)/shard_map/ppermute | solution.py:424
  45.1 0.7 copy-done.3
  45.8 2.2 %regroup.1 = (f32[4,64,128]{2,1,0:T(8,128)}, f32[4,64,128]{2,1,0:T(8,128)}, f32[4,64,128]{2,1,0:T(8,128)}, f32[4,64,128]{2,1,0:T(8,128)}, f32[4,64,128]{2,1,0:T(...) custom-call(f32[8,64,128]{2,1,0:T(8,128)} %bitcast.10, f32[8,64,128]{2,1,0:T(8,128)} %copy-done.1, ...), custom_call_target="tpu_custom_call" | custom-call | tf_op jit(solution)/shard_map/regroup/pallas_call | solution.py:412
  48.0 0.8 collective-permute-start.3
  48.9 1.2 collective-permute-start.4
  50.1 0.5 collective-permute-start.5
  50.5 2.7 %collective-permute-start.7 = (f32[4,64,128]{2,1,0:T(8,128)}, f32[4,64,128]{2,1,0:T(8,128)S(1)}, u32[]{:S(2)}, u32[]{:S(2)}) collective-permute-start(f32[4,64,128]{2,1,0:T(8,128)} %get-tuple-element.43), channel_id=1, source_target_pairs={{0,5},{1,4},{2,7},{3,6},{4,1},{5,0},{6,3},{7,2},{8,13},{9,12},{10,... | collective-permute-start | bytes 393224 | tf_op jit(solution)/shard_map/ppermute | solution.py:424
  53.3 0.4 collective-permute-start.8
  53.7 0.5 collective-permute-done.4.refs_2_
  54.1 3.9 %collective-permute-start.9 = (f32[4,64,128]{2,1,0:T(8,128)}, f32[4,64,128]{2,1,0:T(8,128)S(1)}, u32[]{:S(2)}, u32[]{:S(2)}) collective-permute-start(f32[4,64,128]{2,1,0:T(8,128)} %get-tuple-element.45), channel_id=1, source_target_pairs={{0,7},{1,6},{2,5},{3,4},{4,3},{5,2},{6,1},{7,0},{8,15},{9,14},{10,... | collective-permute-start | bytes 393224 | tf_op jit(solution)/shard_map/ppermute | solution.py:424
  58.0 0.1 cosine_bitcast_fusion
  58.1 0.6 concatenate.3.refs_9_.refs_2_
  58.7 0.5 collective-permute-done.5.refs_3_
  59.2 0.7 collective-permute-done.6.refs_4_
  59.9 3.5 %collective-permute-done.7.refs_5_ = f32[4,64,128]{2,1,0:T(8,128)S(1)} collective-permute-done((f32[4,64,128]{2,1,0:T(8,128)}, f32[4,64,128]{2,1,0:T(8,128)S(1)}, u32[]{:S(2)}, u32[]{:S(2)}) %collective-permute-start.7) | collective-permute-done | bytes 131104 | tf_op jit(solution)/shard_map/ppermute | solution.py:424
  63.4 10.0 %collective-permute-done.8.refs_6_ = f32[4,64,128]{2,1,0:T(8,128)S(1)} collective-permute-done((f32[4,64,128]{2,1,0:T(8,128)}, f32[4,64,128]{2,1,0:T(8,128)S(1)}, u32[]{:S(2)}, u32[]{:S(2)}) %collective-permute-start.8) | collective-permute-done | bytes 131104 | tf_op jit(solution)/shard_map/ppermute | solution.py:424
  73.4 3.2 %collective-permute-done.9.refs_7_ = f32[4,64,128]{2,1,0:T(8,128)S(1)} collective-permute-done((f32[4,64,128]{2,1,0:T(8,128)}, f32[4,64,128]{2,1,0:T(8,128)S(1)}, u32[]{:S(2)}, u32[]{:S(2)}) %collective-permute-start.9) | collective-permute-done | bytes 131104 | tf_op jit(solution)/shard_map/ppermute | solution.py:424
  76.6 0.6 copy-done.20
  77.2 8.0 %middle.2 = (f32[2,128,128]{2,1,0:T(8,128)}, f32[2,128,128]{2,1,0:T(8,128)}, f32[2,128,128]{2,1,0:T(8,128)}, f32[2,128,128]{2,1,0:T(8,128)}, f32[2,128,128]{2,1,...) custom-call(f32[4,64,128]{2,1,0:T(8,128)} %get-tuple-element.38.refs_0_, ...), custom_call_target="tpu_custom_call" | custom-call | tf_op jit(solution)/shard_map/middle/pallas_call | solution.py:390
  85.2 0.0 collective-permute-start.10
  85.3 0.1 collective-permute-start.11
  85.4 1.0 copy-done
  86.4 7.8 %middle.3 = (f32[2,128,128]{2,1,0:T(8,128)}, f32[2,128,128]{2,1,0:T(8,128)}, f32[2,128,128]{2,1,0:T(8,128)}, f32[2,128,128]{2,1,0:T(8,128)}, f32[2,128,128]{2,1,...) custom-call(f32[32,64,128]{2,1,0:T(8,128)} %copy-done, f32[1024,128]{1,0:T(8,128)} %refs_1_.1, ...), custom_call_target="tpu_custom_call" | custom-call | tf_op jit(solution)/shard_map/middle/pallas_call | solution.py:390
  94.2 0.5 collective-permute-start.17
  94.7 1.7 %collective-permute-start.18 = (f32[2,128,128]{2,1,0:T(8,128)}, f32[2,128,128]{2,1,0:T(8,128)S(1)}, u32[]{:S(2)}, u32[]{:S(2)}) collective-permute-start(f32[2,128,128]{2,1,0:T(8,128)} %get-tuple-element.57), channel_id=1, source_target_pairs={{0,2},{1,3},{2,0},{3,1},{4,6},{5,7},{6,4},{7,5},{8,10},{9,11},{10,... | collective-permute-start | bytes 393224 | tf_op jit(solution)/shard_map/ppermute | solution.py:424
  96.4 1.1 collective-permute-start.20
  97.5 1.8 %collective-permute-start.21 = (f32[2,128,128]{2,1,0:T(8,128)}, f32[2,128,128]{2,1,0:T(8,128)S(1)}, u32[]{:S(2)}, u32[]{:S(2)}) collective-permute-start(f32[2,128,128]{2,1,0:T(8,128)} %get-tuple-element.60), channel_id=1, source_target_pairs={{0,5},{1,4},{2,7},{3,6},{4,1},{5,0},{6,3},{7,2},{8,13},{9,12},{10,... | collective-permute-start | bytes 393224 | tf_op jit(solution)/shard_map/ppermute | solution.py:424
  99.3 0.1 collective-permute-start.22
  99.4 1.0 collective-permute-done.18.refs_2_
  100.4 4.3 %collective-permute-start.23 = (f32[2,128,128]{2,1,0:T(8,128)}, f32[2,128,128]{2,1,0:T(8,128)S(1)}, u32[]{:S(2)}, u32[]{:S(2)}) collective-permute-start(f32[2,128,128]{2,1,0:T(8,128)} %get-tuple-element.62), channel_id=1, source_target_pairs={{0,7},{1,6},{2,5},{3,4},{4,3},{5,2},{6,1},{7,0},{8,15},{9,14},{10,... | collective-permute-start | bytes 393224 | tf_op jit(solution)/shard_map/ppermute | solution.py:424
  104.7 2.1 %collective-permute-start.12 = (f32[2,128,128]{2,1,0:T(8,128)S(1)}, f32[2,128,128]{2,1,0:T(8,128)S(1)}, u32[]{:S(2)}, u32[]{:S(2)}) collective-permute-start(f32[2,128,128]{2,1,0:T(8,128)S(1)} %copy-done.33), channel_id=1, source_target_pairs={{0,3},{1,2},{2,1},{3,0},{4,7},{5,6},{6,5},{7,4},{8,11},{9,10},{10,... | collective-permute-start | bytes 393224 | tf_op jit(solution)/shard_map/ppermute | solution.py:424
  106.8 1.8 %collective-permute-start.13 = (f32[2,128,128]{2,1,0:T(8,128)S(1)}, f32[2,128,128]{2,1,0:T(8,128)S(1)}, u32[]{:S(2)}, u32[]{:S(2)}) collective-permute-start(f32[2,128,128]{2,1,0:T(8,128)S(1)} %copy-done.32), channel_id=1, source_target_pairs={{0,4},{1,5},{2,6},{3,7},{4,0},{5,1},{6,2},{7,3},{8,12},{9,13},{10,... | collective-permute-start | bytes 393224 | tf_op jit(solution)/shard_map/ppermute | solution.py:424
  108.6 6.1 %collective-permute-done.21.refs_5_ = f32[2,128,128]{2,1,0:T(8,128)S(1)} collective-permute-done((f32[2,128,128]{2,1,0:T(8,128)}, f32[2,128,128]{2,1,0:T(8,128)S(1)}, u32[]{:S(2)}, u32[]{:S(2)}) %collective-permute-start.21) | collective-permute-done | bytes 131104 | tf_op jit(solution)/shard_map/ppermute | solution.py:424
  114.7 3.5 %collective-permute-start.14 = (f32[2,128,128]{2,1,0:T(8,128)S(1)}, f32[2,128,128]{2,1,0:T(8,128)S(1)}, u32[]{:S(2)}, u32[]{:S(2)}) collective-permute-start(f32[2,128,128]{2,1,0:T(8,128)S(1)} %copy-done.31), channel_id=1, source_target_pairs={{0,5},{1,4},{2,7},{3,6},{4,1},{5,0},{6,3},{7,2},{8,13},{9,12},{10,... | collective-permute-start | bytes 393224 | tf_op jit(solution)/shard_map/ppermute | solution.py:424
  118.1 7.3 %collective-permute-done.22.refs_6_ = f32[2,128,128]{2,1,0:T(8,128)S(1)} collective-permute-done((f32[2,128,128]{2,1,0:T(8,128)}, f32[2,128,128]{2,1,0:T(8,128)S(1)}, u32[]{:S(2)}, u32[]{:S(2)}) %collective-permute-start.22) | collective-permute-done | bytes 131104 | tf_op jit(solution)/shard_map/ppermute | solution.py:424
  125.5 9.4 %collective-permute-done.23.refs_7_ = f32[2,128,128]{2,1,0:T(8,128)S(1)} collective-permute-done((f32[2,128,128]{2,1,0:T(8,128)}, f32[2,128,128]{2,1,0:T(8,128)S(1)}, u32[]{:S(2)}, u32[]{:S(2)}) %collective-permute-start.23) | collective-permute-done | bytes 131104 | tf_op jit(solution)/shard_map/ppermute | solution.py:424
  134.9 0.6 copy-done.22
  135.5 2.6 %final.2.refs_8_ = f32[4,128,1024]{2,1,0:T(8,128)} custom-call(f32[2,128,128]{2,1,0:T(8,128)} %get-tuple-element.55.refs_0_, f32[2,128,128]{2,1,0:T(8,128)} %copy-done.8, f32[2,128,128]{2,1,0:T(8,128)} %copy-done.9, f32[2,128,128]{2,1,0:T(8,128)} %copy-done.10, f32[2,128,128]{2,1,0:T(8,128)} %copy-done.13, f32[2,128,128]{2,1,0:T(8,128)} %copy-done.16, ...), custom_call_target="tpu_custom_call" | custom-call | tf_op jit(solution)/shard_map/final/pallas_call | solution.py:467
  138.1 4.2 %collective-permute-done.15.refs_6_ = f32[2,128,128]{2,1,0:T(8,128)S(1)} collective-permute-done((f32[2,128,128]{2,1,0:T(8,128)S(1)}, f32[2,128,128]{2,1,0:T(8,128)S(1)}, u32[]{:S(2)}, u32[]{:S(2)}) %collective-permute-start.15) | collective-permute-done | bytes 131104 | tf_op jit(solution)/shard_map/ppermute | solution.py:424
  142.3 3.1 %collective-permute-done.16.refs_7_ = f32[2,128,128]{2,1,0:T(8,128)S(1)} collective-permute-done((f32[2,128,128]{2,1,0:T(8,128)S(1)}, f32[2,128,128]{2,1,0:T(8,128)S(1)}, u32[]{:S(2)}, u32[]{:S(2)}) %collective-permute-start.16) | collective-permute-done | bytes 131104 | tf_op jit(solution)/shard_map/ppermute | solution.py:424
  145.5 0.6 copy-done.24
  146.1 2.6 %final.3 = f32[4,128,1024]{2,1,0:T(8,128)} custom-call(f32[2,128,128]{2,1,0:T(8,128)} %get-tuple-element.46.refs_0_, f32[2,128,128]{2,1,0:T(8,128)} %copy-done.4, f32[2,128,128]{2,1,0:T(8,128)} %copy-done.5, f32[2,128,128]{2,1,0:T(8,128)} %copy-done.15, f32[2,128,128]{2,1,0:T(8,128)} %copy-done.18, ...), custom_call_target="tpu_custom_call", output_to_operand_aliasing={{}: (8, {})} | custom-call | tf_op jit(solution)/shard_map/final/pallas_call | solution.py:467
  (82 shorter events, 0.2 us)
Async XLA Ops:
  13.1 7.5 %copy-start.27 = (f32[8,4,2,8,128]{4,3,2,1,0:T(8,128)S(1)}, f32[8,4,2,8,128]{4,3,2,1,0:T(8,128)}, u32[]{:S(2)}) copy-start(f32[8,4,2,8,128]{4,3,2,1,0:T(8,128)} %get-tuple-element.36) | copy-start | bytes 786436
  13.1 8.8 %copy-start.26 = (f32[8,4,2,8,128]{4,3,2,1,0:T(8,128)S(1)}, f32[8,4,2,8,128]{4,3,2,1,0:T(8,128)}, u32[]{:S(2)}) copy-start(f32[8,4,2,8,128]{4,3,2,1,0:T(8,128)} %get-tuple-element.37) | copy-start | bytes 786436
  13.1 44.9 %copy-start.25 = (s32[3,128]{1,0:T(4,128)S(1)}, s32[3,128]{1,0:T(4,128)}, u32[]{:S(2)}) copy-start(s32[3,128]{1,0:T(4,128)} %constant.38.clone) | copy-start | bytes 4612
  13.1 72.3 %all-to-all-start = ((f32[32,64,128]{2,1,0:T(8,128)}), f32[32,64,128]{2,1,0:T(8,128)S(1)}, u32[]{:S(2)}, u32[]{:S(2)}) async-start(f32[32,64,128]{2,1,0:T(8,128)} %bitcast.8), calls=%async_computation | async-start | bytes 2097152 | tf_op jit(solution)/shard_map/all_to_all | solution.py:501
  19.3 16.4 %collective-permute-start = (f32[8,64,128]{2,1,0:T(8,128)S(1)}, f32[8,64,128]{2,1,0:T(8,128)S(1)}, u32[]{:S(2)}, u32[]{:S(2)}) collective-permute-start(f32[8,64,128]{2,1,0:T(8,128)S(1)} %bitcast.13), channel_id=1, source_target_pairs={{0,8},{8,0},{16,24},{24,16},{1,9},{9,1},{17,25},{25,17},{2,10},{10... | collective-permute-start | bytes 786440 | tf_op jit(solution)/shard_map/ppermute | solution.py:424
  20.6 15.2 %collective-permute-start.1 = (f32[8,64,128]{2,1,0:T(8,128)S(1)}, f32[8,64,128]{2,1,0:T(8,128)S(1)}, u32[]{:S(2)}, u32[]{:S(2)}) collective-permute-start(f32[8,64,128]{2,1,0:T(8,128)S(1)} %bitcast.12), channel_id=1, source_target_pairs={{0,16},{8,24},{16,0},{24,8},{1,17},{9,25},{17,1},{25,9},{2,18},{10... | collective-permute-start | bytes 786440 | tf_op jit(solution)/shard_map/ppermute | solution.py:424
  21.8 23.3 %collective-permute-start.2 = (f32[8,64,128]{2,1,0:T(8,128)S(1)}, f32[8,64,128]{2,1,0:T(8,128)S(1)}, u32[]{:S(2)}, u32[]{:S(2)}) collective-permute-start(f32[8,64,128]{2,1,0:T(8,128)S(1)} %bitcast.11), channel_id=1, source_target_pairs={{0,24},{8,16},{16,8},{24,0},{1,25},{9,17},{17,9},{25,1},{2,26},{10... | collective-permute-start | bytes 786440 | tf_op jit(solution)/shard_map/ppermute | solution.py:424
  35.8 9.3 %copy-start.1 = (f32[8,64,128]{2,1,0:T(8,128)}, f32[8,64,128]{2,1,0:T(8,128)S(1)}, u32[]{:S(2)}) copy-start(f32[8,64,128]{2,1,0:T(8,128)S(1)} %collective-permute-done.refs_1_) | copy-start | bytes 786436
  35.8 9.3 %copy-start.2 = (f32[8,64,128]{2,1,0:T(8,128)}, f32[8,64,128]{2,1,0:T(8,128)S(1)}, u32[]{:S(2)}) copy-start(f32[8,64,128]{2,1,0:T(8,128)S(1)} %collective-permute-done.1.refs_2_) | copy-start | bytes 786436
  48.0 5.2 %collective-permute-start.3 = (f32[4,64,128]{2,1,0:T(8,128)}, f32[4,64,128]{2,1,0:T(8,128)S(1)}, u32[]{:S(2)}, u32[]{:S(2)}) collective-permute-start(f32[4,64,128]{2,1,0:T(8,128)} %get-tuple-element.39), channel_id=1, source_target_pairs={{0,1},{1,0},{2,3},{3,2},{4,5},{5,4},{6,7},{7,6},{8,9},{9,8},{10,11... | collective-permute-start | bytes 393224 | tf_op jit(solution)/shard_map/ppermute | solution.py:424
  48.9 5.2 %collective-permute-start.4 = (f32[4,64,128]{2,1,0:T(8,128)}, f32[4,64,128]{2,1,0:T(8,128)S(1)}, u32[]{:S(2)}, u32[]{:S(2)}) collective-permute-start(f32[4,64,128]{2,1,0:T(8,128)} %get-tuple-element.40), channel_id=1, source_target_pairs={{0,2},{1,3},{2,0},{3,1},{4,6},{5,7},{6,4},{7,5},{8,10},{9,11},{10,... | collective-permute-start | bytes 393224 | tf_op jit(solution)/shard_map/ppermute | solution.py:424
  50.1 9.1 %collective-permute-start.5 = (f32[4,64,128]{2,1,0:T(8,128)}, f32[4,64,128]{2,1,0:T(8,128)S(1)}, u32[]{:S(2)}, u32[]{:S(2)}) collective-permute-start(f32[4,64,128]{2,1,0:T(8,128)} %get-tuple-element.41), channel_id=1, source_target_pairs={{0,3},{1,2},{2,1},{3,0},{4,7},{5,6},{6,5},{7,4},{8,11},{9,10},{10,... | collective-permute-start | bytes 393224 | tf_op jit(solution)/shard_map/ppermute | solution.py:424
  50.5 9.3 %collective-permute-start.6 = (f32[4,64,128]{2,1,0:T(8,128)}, f32[4,64,128]{2,1,0:T(8,128)S(1)}, u32[]{:S(2)}, u32[]{:S(2)}) collective-permute-start(f32[4,64,128]{2,1,0:T(8,128)} %get-tuple-element.42), channel_id=1, source_target_pairs={{0,4},{1,5},{2,6},{3,7},{4,0},{5,1},{6,2},{7,3},{8,12},{9,13},{10,... | collective-permute-start | bytes 393224 | tf_op jit(solution)/shard_map/ppermute | solution.py:424
  50.5 12.9 %collective-permute-start.7 = (f32[4,64,128]{2,1,0:T(8,128)}, f32[4,64,128]{2,1,0:T(8,128)S(1)}, u32[]{:S(2)}, u32[]{:S(2)}) collective-permute-start(f32[4,64,128]{2,1,0:T(8,128)} %get-tuple-element.43), channel_id=1, source_target_pairs={{0,5},{1,4},{2,7},{3,6},{4,1},{5,0},{6,3},{7,2},{8,13},{9,12},{10,... | collective-permute-start | bytes 393224 | tf_op jit(solution)/shard_map/ppermute | solution.py:424
  53.3 23.3 %copy-start.6 = (f32[4,64,128]{2,1,0:T(8,128)}, f32[4,64,128]{2,1,0:T(8,128)S(1)}, u32[]{:S(2)}) copy-start(f32[4,64,128]{2,1,0:T(8,128)S(1)} %collective-permute-done.3.refs_1_) | copy-start | bytes 393220
  53.3 20.1 %collective-permute-start.8 = (f32[4,64,128]{2,1,0:T(8,128)}, f32[4,64,128]{2,1,0:T(8,128)S(1)}, u32[]{:S(2)}, u32[]{:S(2)}) collective-permute-start(f32[4,64,128]{2,1,0:T(8,128)} %get-tuple-element.44), channel_id=1, source_target_pairs={{0,6},{1,7},{2,4},{3,5},{4,2},{5,3},{6,0},{7,1},{8,14},{9,15},{10,... | collective-permute-start | bytes 393224 | tf_op jit(solution)/shard_map/ppermute | solution.py:424
  54.1 22.5 %copy-start.7 = (f32[4,64,128]{2,1,0:T(8,128)}, f32[4,64,128]{2,1,0:T(8,128)S(1)}, u32[]{:S(2)}) copy-start(f32[4,64,128]{2,1,0:T(8,128)S(1)} %collective-permute-done.4.refs_2_) | copy-start | bytes 393220
  54.1 22.5 %collective-permute-start.9 = (f32[4,64,128]{2,1,0:T(8,128)}, f32[4,64,128]{2,1,0:T(8,128)S(1)}, u32[]{:S(2)}, u32[]{:S(2)}) collective-permute-start(f32[4,64,128]{2,1,0:T(8,128)} %get-tuple-element.45), channel_id=1, source_target_pairs={{0,7},{1,6},{2,5},{3,4},{4,3},{5,2},{6,1},{7,0},{8,15},{9,14},{10,... | collective-permute-start | bytes 393224 | tf_op jit(solution)/shard_map/ppermute | solution.py:424
  59.2 17.4 %copy-start.11 = (f32[4,64,128]{2,1,0:T(8,128)}, f32[4,64,128]{2,1,0:T(8,128)S(1)}, u32[]{:S(2)}) copy-start(f32[4,64,128]{2,1,0:T(8,128)S(1)} %collective-permute-done.5.refs_3_) | copy-start | bytes 393220
  59.9 16.7 %copy-start.12 = (f32[4,64,128]{2,1,0:T(8,128)}, f32[4,64,128]{2,1,0:T(8,128)S(1)}, u32[]{:S(2)}) copy-start(f32[4,64,128]{2,1,0:T(8,128)S(1)} %collective-permute-done.6.refs_4_) | copy-start | bytes 393220
  63.4 13.2 %copy-start.14 = (f32[4,64,128]{2,1,0:T(8,128)}, f32[4,64,128]{2,1,0:T(8,128)S(1)}, u32[]{:S(2)}) copy-start(f32[4,64,128]{2,1,0:T(8,128)S(1)} %collective-permute-done.7.refs_5_) | copy-start | bytes 393220
  85.2 11.2 %collective-permute-start.10 = (f32[2,128,128]{2,1,0:T(8,128)}, f32[2,128,128]{2,1,0:T(8,128)S(1)}, u32[]{:S(2)}, u32[]{:S(2)}) collective-permute-start(f32[2,128,128]{2,1,0:T(8,128)} %get-tuple-element.47), channel_id=1, source_target_pairs={{0,1},{1,0},{2,3},{3,2},{4,5},{5,4},{6,7},{7,6},{8,9},{9,8},{10,11... | collective-permute-start | bytes 393224 | tf_op jit(solution)/shard_map/ppermute | solution.py:424
  85.3 19.4 %copy-start.33 = (f32[2,128,128]{2,1,0:T(8,128)S(1)}, f32[2,128,128]{2,1,0:T(8,128)}, u32[]{:S(2)}) copy-start(f32[2,128,128]{2,1,0:T(8,128)} %get-tuple-element.49) | copy-start | bytes 393220
  85.3 21.5 %copy-start.32 = (f32[2,128,128]{2,1,0:T(8,128)S(1)}, f32[2,128,128]{2,1,0:T(8,128)}, u32[]{:S(2)}) copy-start(f32[2,128,128]{2,1,0:T(8,128)} %get-tuple-element.50) | copy-start | bytes 393220
  85.3 29.4 %copy-start.31 = (f32[2,128,128]{2,1,0:T(8,128)S(1)}, f32[2,128,128]{2,1,0:T(8,128)}, u32[]{:S(2)}) copy-start(f32[2,128,128]{2,1,0:T(8,128)} %get-tuple-element.51) | copy-start | bytes 393220
  85.3 40.2 %copy-start.30 = (f32[2,128,128]{2,1,0:T(8,128)S(1)}, f32[2,128,128]{2,1,0:T(8,128)}, u32[]{:S(2)}) copy-start(f32[2,128,128]{2,1,0:T(8,128)} %get-tuple-element.52) | copy-start | bytes 393220
  85.3 49.5 %copy-start.29 = (f32[2,128,128]{2,1,0:T(8,128)S(1)}, f32[2,128,128]{2,1,0:T(8,128)}, u32[]{:S(2)}) copy-start(f32[2,128,128]{2,1,0:T(8,128)} %get-tuple-element.53) | copy-start | bytes 393220
  85.3 12.2 %collective-permute-start.11 = (f32[2,128,128]{2,1,0:T(8,128)}, f32[2,128,128]{2,1,0:T(8,128)S(1)}, u32[]{:S(2)}, u32[]{:S(2)}) collective-permute-start(f32[2,128,128]{2,1,0:T(8,128)} %get-tuple-element.48), channel_id=1, source_target_pairs={{0,2},{1,3},{2,0},{3,1},{4,6},{5,7},{6,4},{7,5},{8,10},{9,11},{10,... | collective-permute-start | bytes 393224 | tf_op jit(solution)/shard_map/ppermute | solution.py:424
  94.2 5.2 %collective-permute-start.17 = (f32[2,128,128]{2,1,0:T(8,128)}, f32[2,128,128]{2,1,0:T(8,128)S(1)}, u32[]{:S(2)}, u32[]{:S(2)}) collective-permute-start(f32[2,128,128]{2,1,0:T(8,128)} %get-tuple-element.56), channel_id=1, source_target_pairs={{0,1},{1,0},{2,3},{3,2},{4,5},{5,4},{6,7},{7,6},{8,9},{9,8},{10,11... | collective-permute-start | bytes 393224 | tf_op jit(solution)/shard_map/ppermute | solution.py:424
  94.7 5.7 %collective-permute-start.18 = (f32[2,128,128]{2,1,0:T(8,128)}, f32[2,128,128]{2,1,0:T(8,128)S(1)}, u32[]{:S(2)}, u32[]{:S(2)}) collective-permute-start(f32[2,128,128]{2,1,0:T(8,128)} %get-tuple-element.57), channel_id=1, source_target_pairs={{0,2},{1,3},{2,0},{3,1},{4,6},{5,7},{6,4},{7,5},{8,10},{9,11},{10,... | collective-permute-start | bytes 393224 | tf_op jit(solution)/shard_map/ppermute | solution.py:424
  96.4 8.3 %collective-permute-start.19 = (f32[2,128,128]{2,1,0:T(8,128)}, f32[2,128,128]{2,1,0:T(8,128)S(1)}, u32[]{:S(2)}, u32[]{:S(2)}) collective-permute-start(f32[2,128,128]{2,1,0:T(8,128)} %get-tuple-element.58), channel_id=1, source_target_pairs={{0,3},{1,2},{2,1},{3,0},{4,7},{5,6},{6,5},{7,4},{8,11},{9,10},{10,... | collective-permute-start | bytes 393224 | tf_op jit(solution)/shard_map/ppermute | solution.py:424
  96.4 49.0 %copy-start.4 = (f32[2,128,128]{2,1,0:T(8,128)}, f32[2,128,128]{2,1,0:T(8,128)S(1)}, u32[]{:S(2)}) copy-start(f32[2,128,128]{2,1,0:T(8,128)S(1)} %collective-permute-done.10.refs_1_) | copy-start | bytes 393220
  96.4 10.4 %collective-permute-start.20 = (f32[2,128,128]{2,1,0:T(8,128)}, f32[2,128,128]{2,1,0:T(8,128)S(1)}, u32[]{:S(2)}, u32[]{:S(2)}) collective-permute-start(f32[2,128,128]{2,1,0:T(8,128)} %get-tuple-element.59), channel_id=1, source_target_pairs={{0,4},{1,5},{2,6},{3,7},{4,0},{5,1},{6,2},{7,3},{8,12},{9,13},{10,... | collective-permute-start | bytes 393224 | tf_op jit(solution)/shard_map/ppermute | solution.py:424
  97.5 47.9 %copy-start.5 = (f32[2,128,128]{2,1,0:T(8,128)}, f32[2,128,128]{2,1,0:T(8,128)S(1)}, u32[]{:S(2)}) copy-start(f32[2,128,128]{2,1,0:T(8,128)S(1)} %collective-permute-done.11.refs_2_) | copy-start | bytes 393220
  97.5 17.1 %collective-permute-start.21 = (f32[2,128,128]{2,1,0:T(8,128)}, f32[2,128,128]{2,1,0:T(8,128)S(1)}, u32[]{:S(2)}, u32[]{:S(2)}) collective-permute-start(f32[2,128,128]{2,1,0:T(8,128)} %get-tuple-element.60), channel_id=1, source_target_pairs={{0,5},{1,4},{2,7},{3,6},{4,1},{5,0},{6,3},{7,2},{8,13},{9,12},{10,... | collective-permute-start | bytes 393224 | tf_op jit(solution)/shard_map/ppermute | solution.py:424
  99.3 35.5 %copy-start.8 = (f32[2,128,128]{2,1,0:T(8,128)}, f32[2,128,128]{2,1,0:T(8,128)S(1)}, u32[]{:S(2)}) copy-start(f32[2,128,128]{2,1,0:T(8,128)S(1)} %collective-permute-done.17.refs_1_) | copy-start | bytes 393220
  99.3 26.1 %collective-permute-start.22 = (f32[2,128,128]{2,1,0:T(8,128)}, f32[2,128,128]{2,1,0:T(8,128)S(1)}, u32[]{:S(2)}, u32[]{:S(2)}) collective-permute-start(f32[2,128,128]{2,1,0:T(8,128)} %get-tuple-element.61), channel_id=1, source_target_pairs={{0,6},{1,7},{2,4},{3,5},{4,2},{5,3},{6,0},{7,1},{8,14},{9,15},{10,... | collective-permute-start | bytes 393224 | tf_op jit(solution)/shard_map/ppermute | solution.py:424
  100.4 34.5 %copy-start.9 = (f32[2,128,128]{2,1,0:T(8,128)}, f32[2,128,128]{2,1,0:T(8,128)S(1)}, u32[]{:S(2)}) copy-start(f32[2,128,128]{2,1,0:T(8,128)S(1)} %collective-permute-done.18.refs_2_) | copy-start | bytes 393220
  100.4 34.5 %collective-permute-start.23 = (f32[2,128,128]{2,1,0:T(8,128)}, f32[2,128,128]{2,1,0:T(8,128)S(1)}, u32[]{:S(2)}, u32[]{:S(2)}) collective-permute-start(f32[2,128,128]{2,1,0:T(8,128)} %get-tuple-element.62), channel_id=1, source_target_pairs={{0,7},{1,6},{2,5},{3,4},{4,3},{5,2},{6,1},{7,0},{8,15},{9,14},{10,... | collective-permute-start | bytes 393224 | tf_op jit(solution)/shard_map/ppermute | solution.py:424
  104.6 30.2 %copy-start.10 = (f32[2,128,128]{2,1,0:T(8,128)}, f32[2,128,128]{2,1,0:T(8,128)S(1)}, u32[]{:S(2)}) copy-start(f32[2,128,128]{2,1,0:T(8,128)S(1)} %collective-permute-done.19.refs_3_) | copy-start | bytes 393220
  104.7 33.4 %collective-permute-start.12 = (f32[2,128,128]{2,1,0:T(8,128)S(1)}, f32[2,128,128]{2,1,0:T(8,128)S(1)}, u32[]{:S(2)}, u32[]{:S(2)}) collective-permute-start(f32[2,128,128]{2,1,0:T(8,128)S(1)} %copy-done.33), channel_id=1, source_target_pairs={{0,3},{1,2},{2,1},{3,0},{4,7},{5,6},{6,5},{7,4},{8,11},{9,10},{10,... | collective-permute-start | bytes 393224 | tf_op jit(solution)/shard_map/ppermute | solution.py:424
  106.8 28.1 %copy-start.13 = (f32[2,128,128]{2,1,0:T(8,128)}, f32[2,128,128]{2,1,0:T(8,128)S(1)}, u32[]{:S(2)}) copy-start(f32[2,128,128]{2,1,0:T(8,128)S(1)} %collective-permute-done.20.refs_4_) | copy-start | bytes 393220
  106.8 31.3 %collective-permute-start.13 = (f32[2,128,128]{2,1,0:T(8,128)S(1)}, f32[2,128,128]{2,1,0:T(8,128)S(1)}, u32[]{:S(2)}, u32[]{:S(2)}) collective-permute-start(f32[2,128,128]{2,1,0:T(8,128)S(1)} %copy-done.32), channel_id=1, source_target_pairs={{0,4},{1,5},{2,6},{3,7},{4,0},{5,1},{6,2},{7,3},{8,12},{9,13},{10,... | collective-permute-start | bytes 393224 | tf_op jit(solution)/shard_map/ppermute | solution.py:424
  114.7 20.2 %copy-start.16 = (f32[2,128,128]{2,1,0:T(8,128)}, f32[2,128,128]{2,1,0:T(8,128)S(1)}, u32[]{:S(2)}) copy-start(f32[2,128,128]{2,1,0:T(8,128)S(1)} %collective-permute-done.21.refs_5_) | copy-start | bytes 393220
  114.7 23.4 %collective-permute-start.14 = (f32[2,128,128]{2,1,0:T(8,128)S(1)}, f32[2,128,128]{2,1,0:T(8,128)S(1)}, u32[]{:S(2)}, u32[]{:S(2)}) collective-permute-start(f32[2,128,128]{2,1,0:T(8,128)S(1)} %copy-done.31), channel_id=1, source_target_pairs={{0,5},{1,4},{2,7},{3,6},{4,1},{5,0},{6,3},{7,2},{8,13},{9,12},{10,... | collective-permute-start | bytes 393224 | tf_op jit(solution)/shard_map/ppermute | solution.py:424
  125.5 9.5 %copy-start.19 = (f32[2,128,128]{2,1,0:T(8,128)}, f32[2,128,128]{2,1,0:T(8,128)S(1)}, u32[]{:S(2)}) copy-start(f32[2,128,128]{2,1,0:T(8,128)S(1)} %collective-permute-done.22.refs_6_) | copy-start | bytes 393220
  125.5 16.8 %collective-permute-start.15 = (f32[2,128,128]{2,1,0:T(8,128)S(1)}, f32[2,128,128]{2,1,0:T(8,128)S(1)}, u32[]{:S(2)}, u32[]{:S(2)}) collective-permute-start(f32[2,128,128]{2,1,0:T(8,128)S(1)} %copy-done.30), channel_id=1, source_target_pairs={{0,6},{1,7},{2,4},{3,5},{4,2},{5,3},{6,0},{7,1},{8,14},{9,15},{10,... | collective-permute-start | bytes 393224 | tf_op jit(solution)/shard_map/ppermute | solution.py:424
  134.9 10.6 %collective-permute-start.16 = (f32[2,128,128]{2,1,0:T(8,128)S(1)}, f32[2,128,128]{2,1,0:T(8,128)S(1)}, u32[]{:S(2)}, u32[]{:S(2)}) collective-permute-start(f32[2,128,128]{2,1,0:T(8,128)S(1)} %copy-done.29), channel_id=1, source_target_pairs={{0,7},{1,6},{2,5},{3,4},{4,3},{5,2},{6,1},{7,0},{8,15},{9,14},{10,... | collective-permute-start | bytes 393224 | tf_op jit(solution)/shard_map/ppermute | solution.py:424
  (11 other events, 38.5 us)

commit v2 on v1

--- a/solution.py
+++ b/solution.py
@@ -51,8 +51,9 @@
         self.small = 2 ** (self.t_low + len(self.q_in))
         assert self.small == 8 and n_col == self.major and slots // 2 == 4 * LANES
         self.src_rows = self.rows_rw * 2 * self.small
-        self.q_stack = LANES // self.src_rows
-        self.q_rest = 2 ** len(self.own_q) // self.q_stack
+        self.group = self.rows_rw * self.small
+        self.spare = LANES // self.group // 4
+        self.own_qs = 2 ** len(self.own_q)
         self.w_extra = 2 ** len(self.own_w) // 8
         assert self.w_extra * self.w_kept == 2
         assert self.pairs in (1, 2)
@@ -103,11 +104,10 @@
         return table.reshape(4 * LANES, 4 * LANES)
 
     def y_rows(self):
-        shape = (2, self.q_rest, 4, self.q_stack, self.small)
-        y0, q_rest, y21, q_stack, small = np.indices(shape)
+        y0, own, y21, small = np.indices((2, self.own_qs, 4, self.small))
         n_in = len(self.q_in)
         t_low, q_in = small >> n_in, small & (2 ** n_in - 1)
-        q_local = q_in * 2 ** len(self.own_q) + q_rest * self.q_stack + q_stack
+        q_local = q_in * self.own_qs + own
         return (t_low * LANES + q_local * 8 + y21 * 2 + y0).reshape(-1)
 
     def m_rows(self):
@@ -162,10 +162,6 @@
     return jnp.dot(a, b, preferred_element_type=F32)
 
 
-def dot_nt(a, b):
-    return lax.dot_general(a, b, (((1,), (1,)), ((), ())), preferred_element_type=F32)
-
-
 def three(f, a, b):
     return f(a[0], b[0]) + (f(a[0], b[1]) + f(a[1], b[0]))
 
@@ -176,71 +172,90 @@
     return jnp.where(hit(row, col), 1.0, 0.0).astype(BF16)
 
 
-def spread(mixing, rows, row_of, same, fresh):
+def spread(table, rows, row_of, same):
     pick = one_hot((rows, 64), lambda r, c: c == row_of(r))
-    if fresh:
-        wide = one_hot((64, 448), lambda r, c: r == 8 + c // 8)
-        cell = lambda c: c % 8
-    else:
-        wide = one_hot((64, 64), lambda r, c: r == c % 8)
-        cell = lambda c: c // 8
-    table = dot(dot(pick, mixing).astype(BF16), wide)
+    wide = one_hot((64, 448), lambda r, c: r == 8 + c // 8)
+    table = dot(dot(pick, table).astype(BF16), wide)
     row = lax.broadcasted_iota(jnp.int32, table.shape, 0)
     col = lax.broadcasted_iota(jnp.int32, table.shape, 1)
-    return jnp.where(same(row) == cell(col), table, 0.0).astype(BF16)
-
-
-def carry(table, parents):
-    high = parents.astype(BF16)
-    rest = parents - high.astype(F32)
-    mid = rest.astype(BF16)
-    low = (rest - mid.astype(F32)).astype(BF16)
-    return dot(table, high) + (dot(table, mid) + dot(table, low))
+    return jnp.where(same(row) == col % 8, table, 0.0).astype(BF16)
+
+
+def lane_groups(arrays, group):
+    lane = lax.broadcasted_iota(jnp.int32, arrays[0].shape, 1) // group
+    arrays, step = list(arrays), 1
+    while step < len(arrays):
+        low = (lane // step) % 2 == 0
+        for k in range(len(arrays)):
+            if k // step % 2 == 0:
+                a, b = arrays[k], arrays[k + step]
+                arrays[k] = jnp.where(low, a, pltpu.roll(b, group * step, 1))
+                arrays[k + step] = jnp.where(low, pltpu.roll(a, LANES - group * step, 1), b)
+        step *= 2
+    return arrays
 
 
 def expand_kernel(plan, top, one, two, three_ref, mixing, send, *refs):
     count = plan.pairs if plan.pairs == 1 else plan.n_row + 1
     outs = refs[:count]
-    leaf, w2f, w2p, w3f, w3p, joined = refs[count:]
+    leaf, w_one, w_two, w_three, joined = refs[count:]
     step = pl.program_id(0)
 
     @pl.when(step == 0)
     def _():
         mix = mixing[...]
-        w2f[...] = spread(mix, 512, lambda r: r % 64, lambda r: r // 64, True)
-        w2p[...] = spread(mix, 512, lambda r: r % 64, lambda r: r // 64, False)
         child = lambda r: 8 * (4 * (r // 32 % 2) + 2 * (r // 4 % 2) + r % 2)
         cell = lambda r: 4 * (r // 16 % 2) + 2 * (r // 8 % 2) + r // 2 % 2
-        w3f[...] = spread(mix, 64, child, cell, True)
-        w3p[...] = spread(mix, 64, child, cell, False)
-
-    mix = mixing[...]
-    level = carry(mix[:, :8], top[...]) + dot(mix[:, 8:], one[...])
+        w_three[...] = spread(mix, 64, child, cell)
+        last = dot(dot(one_hot((64, 64), lambda r, c: c == child(r)), mix).astype(BF16), one_hot((64, 64), lambda r, c: r == c % 8))
+        row = lax.broadcasted_iota(jnp.int32, (64, 64), 0)
+        col = lax.broadcasted_iota(jnp.int32, (64, 64), 1)
+        through = dot(jnp.where(cell(row) == col // 8, last, 0.0).astype(BF16), mix)
+        parts = split(through)
+        for k in range(2):
+            w_two[pl.ds(512 * k, 512), :] = spread(parts[k], 512, lambda r: r % 64, lambda r: r // 64)
+        for c in range(8):
+            own = mix[8 * c : 8 * c + 8, :]
+            table = split(dot(parts[0][:, :8], own) + dot(parts[1][:, :8], own))
+            for k in range(2):
+                w_one[pl.ds(64 * c, 64), pl.ds(64 * k, 64)] = table[k]
+
+    upper, lower = split(top[...])
+    ones = jnp.concatenate((upper, one[...]), axis=0)
+    blocks = jnp.concatenate((ones, ones), axis=0)
+    twos = dot(w_two[...], two[...])
+    second = twos[:512] + (twos[512:] + (dot(w_one[...], blocks) + dot(w_one[:, :8], lower)))
     for g in range(8):
-        rows = pl.ds(64 * g, 64)
-        second = dot(w2f[rows, :], two[...]) + carry(w2p[rows, :], level)
         fresh = three_ref[:, pl.ds(8 * g, 8), :].reshape(448, second.shape[1])
-        leaf[g] = dot(w3f[...], fresh) + carry(w3p[...], second)
+        leaf[g] = dot(w_three[...], fresh) + second[64 * g : 64 * g + 64]
     table = (send[0], send[1])
     for x in range(4):
         x2, x1 = x // 2, x % 2
         pair, dest = x % plan.pairs, x // plan.pairs
-        for high in range(2):
-            parts = []
-            for part in range(2):
-                pieces = [
-                    leaf[4 * x2 + yz, pl.ds(32 * part + 16 * x1, 16), pl.ds((2 * high + tau) * LANES, LANES)]
-                    for tau in range(2)
-                    for yz in range(4)
-                ]
-                parts.append(jnp.concatenate(pieces, axis=0))
-            data = split(jnp.concatenate(parts, axis=1))
-            sent = three(dot_nt, table, data)
-            sent = sent.reshape(plan.n_col, plan.rows_rw, plan.small, LANES)
-            if pair == 0:
-                outs[0][0, dest, :, :, high] = sent
-            else:
-                joined[step * plan.dest_x + dest, :, :, high] = sent
+        parts = []
+        for part in range(2):
+            pieces = [
+                leaf[4 * x2 + yz, pl.ds(32 * part + 16 * x1, 16), pl.ds(tile * LANES, LANES)]
+                for tile in range(4)
+                for yz in range(4)
+            ]
+            parts.append(jnp.concatenate(pieces, axis=0))
+        sent = three(dot, split(jnp.concatenate(parts, axis=1)), table)
+        for side in range(2):
+            pieces = []
+            for spare in range(plan.spare):
+                for tau in range(2):
+                    for high in range(2):
+                        start = (2 * high + tau) * 64 + spare * plan.src_rows
+                        pieces.append(
+                            sent[start : start + plan.src_rows, side * LANES : (side + 1) * LANES]
+                        )
+            for k, piece in enumerate(lane_groups(pieces, plan.group)):
+                c = side * (plan.n_col // 2) + k
+                if pair == 0:
+                    outs[0][0, dest, c] = piece
+                else:
+                    joined[step * plan.dest_x + dest, c] = piece
 
     if plan.pairs > 1:
 
@@ -253,34 +268,33 @@
 
 
 def expand(plan, top, one, two, three_in, mixing):
-    half = plan.slots // 2
-    block = (plan.n_col, plan.rows_rw, 2, plan.small, LANES)
+    lanes = plan.slots // 2
+    block = (plan.n_col, plan.src_rows, LANES)
     shapes = [(2, plan.dest_x) + block]
-    specs = [pl.BlockSpec((1, plan.dest_x) + block, lambda i: (i, 0, 0, 0, 0, 0, 0))]
+    specs = [pl.BlockSpec((1, plan.dest_x) + block, lambda i: (i, 0, 0, 0, 0))]
     if plan.pairs > 1:
         shapes += [block] * plan.n_row
-        specs += [pl.BlockSpec(block, lambda i: (0, 0, 0, 0, 0))] * plan.n_row
-    table = halves(plan.send_table())
+        specs += [pl.BlockSpec(block, lambda i: (0, 0, 0))] * plan.n_row
+    table = halves(plan.send_table().T)
     whole = lambda array: pl.BlockSpec(array.shape, lambda i: (0,) * array.ndim)
     return pl.pallas_call(
         functools.partial(expand_kernel, plan),
         grid=(2,),
         in_specs=[
-            pl.BlockSpec((8, half), lambda i: (0, i)),
-            pl.BlockSpec((56, half), lambda i: (0, i)),
-            pl.BlockSpec((448, half), lambda i: (0, i)),
-            pl.BlockSpec((56, 64, half), lambda i: (0, 0, i)),
+            pl.BlockSpec((8, lanes), lambda i: (0, i)),
+            pl.BlockSpec((56, lanes), lambda i: (0, i)),
+            pl.BlockSpec((448, lanes), lambda i: (0, i)),
+            pl.BlockSpec((56, 64, lanes), lambda i: (0, 0, i)),
             whole(mixing),
             whole(table),
         ],
         out_specs=specs,
         out_shape=[jax.ShapeDtypeStruct(shape, F32) for shape in shapes],
         scratch_shapes=[
-            pltpu.VMEM((8, 64, half), F32),
-            pltpu.VMEM((512, 448), BF16),
-            pltpu.VMEM((512, 64), BF16),
+            pltpu.VMEM((8, 64, lanes), F32),
+            pltpu.VMEM((512, 128), BF16),
+            pltpu.VMEM((1024, 448), BF16),
             pltpu.VMEM((64, 448), BF16),
-            pltpu.VMEM((64, 64), BF16),
             pltpu.VMEM((plan.n_row,) + block, F32),
         ],
         compiler_params=pltpu.CompilerParams(vmem_limit_bytes=VMEM_LIMIT),
@@ -304,7 +318,7 @@
     parts, refs = refs[:count], refs[count:]
     factor, lane_turn, z_in, y_in, y_out, turns, z_out = refs[:7]
     outs = refs[7 : 7 + plan.n_col]
-    got, flipped, prep, out = refs[7 + plan.n_col :]
+    got, prep, out = refs[7 + plan.n_col :]
     row, col = lax.axis_index("row"), lax.axis_index("col")
     if count == 1:
         got = parts[0]
@@ -312,31 +326,28 @@
         for shift in range(plan.n_col):
             for far in range(plan.n_row):
                 got[(row ^ far) * plan.n_col + (col ^ shift)] = parts[shift][far]
-    q_tiles = plan.q_rest * 4 * plan.q_stack
-    for q_rest in range(plan.q_rest):
+    q_tiles = plan.own_qs * 4
+    for q in range(plan.own_qs):
         for extra in range(plan.w_extra):
-            for w in range(8):
-                stack = [
-                    got[plan.src(extra * 8 + w, q_rest * plan.q_stack + q)]
-                    for q in range(plan.q_stack)
+            for y21 in range(4 // plan.spare):
+                y2, y1 = y21 // 2, y21 % 2
+                pieces = [
+                    got[plan.src(extra * 8 + w, q), pl.ds(8 * (4 * y2 + 2 * z2 + y1), 8), :]
+                    for w in range(8)
+                    for z2 in range(2)
                 ]
-                flipped[w] = jnp.concatenate(stack, axis=0).T.reshape(16, 8, LANES)
-            for tau in range(2):
-                for y21 in range(4):
-                    y2, y1 = y21 // 2, y21 % 2
-                    pieces = [
-                        flipped[w, 8 * tau + 4 * y2 + 2 * z2 + y1] for w in range(8) for z2 in range(2)
-                    ]
-                    block = jnp.concatenate(pieces, axis=0).T
-                    block = block.reshape(plan.q_stack, 2, plan.w_kept, 2, 8, LANES)
-                    for kept_in in range(plan.w_kept):
-                        kept = extra if plan.w_extra == 2 else kept_in
-                        cos = lane_turn[2 * kept : 2 * kept + 1, :]
-                        sin = lane_turn[2 * kept + 1 : 2 * kept + 2, :]
-                        for q in range(plan.q_stack):
+                block = jnp.concatenate(pieces, axis=0).T
+                block = block.reshape(plan.spare, 2, 2, 2, plan.w_kept, 8, LANES)
+                for kept_in in range(plan.w_kept):
+                    kept = extra if plan.w_extra == 2 else kept_in
+                    cos = lane_turn[2 * kept : 2 * kept + 1, :]
+                    sin = lane_turn[2 * kept + 1 : 2 * kept + 2, :]
+                    for spare in range(plan.spare):
+                        for tau in range(2):
                             for high in range(2):
-                                re, im = block[q, 0, kept_in, high], block[q, 1, kept_in, high]
-                                tile = (2 * high + tau) * q_tiles + (q_rest * 4 + y21) * plan.q_stack + q
+                                re = block[spare, tau, high, 0, kept_in]
+                                im = block[spare, tau, high, 1, kept_in]
+                                tile = (2 * high + tau) * q_tiles + q * 4 + spare * 2 + y21
                                 rows = pl.ds(8 * tile, 8)
                                 prep[rows, pl.ds(2 * kept * LANES, LANES)] = re * cos + im * sin
                                 prep[rows, pl.ds((2 * kept + 1) * LANES, LANES)] = im * cos - re * sin
@@ -392,7 +403,6 @@
         out_shape=[jax.ShapeDtypeStruct((2, LANES, LANES), F32)] * plan.n_col,
         scratch_shapes=[
             pltpu.VMEM((plan.owners, plan.src_rows, LANES), F32),
-            pltpu.VMEM((8, 16, 8, LANES), F32),
             pltpu.VMEM((plan.grid // 2, 4 * LANES), F32),
             pltpu.VMEM((plan.n_col, 2, LANES, LANES), F32),
         ],
@@ -447,18 +457,18 @@
 def final_kernel(plan, *refs):
     parts, out, got = refs[: plan.n_col], refs[-2], refs[-1]
     scale = 1.0 / (plan.grid * plan.grid)
-    step = 16
     col = lax.axis_index("col")
     for shift in range(plan.n_col):
         got[col ^ shift] = parts[shift][...]
-
-    @pl.loop(0, LANES // step)
-    def _(i):
-        rows = pl.ds(pl.multiple_of(i * step, step), step)
+    for tile in range(out.shape[1] // 8):
+        rows = pl.ds(8 * tile, 8)
         parts = [(got[c, 0, rows, :], got[c, 1, rows, :]) for c in range(plan.n_col)]
         for w, (re, im) in enumerate(dft(parts, 1.0)):
             out[0, rows, pl.ds(w * LANES, LANES)] = re * scale
             out[1, rows, pl.ds(w * LANES, LANES)] = im * scale
+
+
+FINAL_ROWS = 64
 
 
 def final(plan, pair, parts, so_far):
@@ -466,12 +476,12 @@
     shape = (plan.planes, LANES, plan.grid)
     return pl.pallas_call(
         functools.partial(final_kernel, plan),
-        grid=(1,),
-        in_specs=[pl.BlockSpec((2, LANES, LANES), lambda i: (0, 0, 0))] * plan.n_col
+        grid=(LANES // FINAL_ROWS,),
+        in_specs=[pl.BlockSpec((2, FINAL_ROWS, LANES), lambda i: (0, i, 0))] * plan.n_col
         + [pl.BlockSpec(memory_space=pl.ANY) for _ in extra],
-        out_specs=pl.BlockSpec((2, LANES, plan.grid), lambda i: (pair, 0, 0)),
+        out_specs=pl.BlockSpec((2, FINAL_ROWS, plan.grid), lambda i: (pair, i, 0)),
         out_shape=jax.ShapeDtypeStruct(shape, F32),
-        scratch_shapes=[pltpu.VMEM((plan.n_col, 2, LANES, LANES), F32)],
+        scratch_shapes=[pltpu.VMEM((plan.n_col, 2, FINAL_ROWS, LANES), F32)],
         input_output_aliases={plan.n_col: 0} if extra else {},
         compiler_params=pltpu.CompilerParams(vmem_limit_bytes=VMEM_LIMIT),
         name="final",

time: 149 us -> 144 us (0.966)
  Pallas kernels: 36.2 us -> 31.3 us
    pallas_call x1, Pallas kernels: 13 us -> 9.51 us  [expand(): pl.pallas_call(functools.partial(expand_kernel, plan), grid=(2,), in_spec...]
where the time goes in v2:
time: 144 us
  waiting for transfers between devices  72.8 us (51%)
  starting transfers between devices  35.4 us (25%)
  Pallas kernels  31.3 us (22%)
  local copies, waits for them, and re-layouts  4.19 us (3%)
    ppermute x24, waiting for transfers between devices, swap(): lax.ppermute(parts[shift], axis, [(k, k ^ shift) for k in range(size)])  72.8 us
    ppermute x24, starting transfers between devices, swap(): lax.ppermute(parts[shift], axis, [(k, k ^ shift) for k in range(size)])  29.2 us
    pallas_call x2, Pallas kernels, middle(): pl.pallas_call(functools.partial(middle_kernel, plan, len(parts)), out_sh...  15.2 us
    pallas_call x1, Pallas kernels, expand(): pl.pallas_call(functools.partial(expand_kernel, plan), grid=(2,), in_spec...  9.51 us
    all_to_all x1, starting transfers between devices, steps(): lax.all_to_all(sent, ('row', 'col'), split_axis=0, concat_axis=0, tiled=T...  6.23 us
    pallas_call x2, Pallas kernels, final(): pl.pallas_call(functools.partial(final_kernel, plan), grid=(LANES // FINA...  4.39 us
    unnamed x68, local copies, waits for them, and re-layouts  3.59 us
  transfers between devices with their start and end apart: 25, of which 14 were waited for; matrix products, arithmetic and copies ran while one was open for 0% of the time, Pallas kernels for 14%

profile of v2, /device:TPU:17, one launch (start us, length us, event | category | flops | bytes accessed | tf_op | source)
XLA Modules:
  0.0 144.1 jit_solution(5283099613461586917)
XLA Ops:
  0.0 9.5 %expand.1 = (f32[2,2,8,64,128]{4,3,2,1,0:T(8,128)}, f32[8,64,128]{2,1,0:T(8,128)}, f32[8,64,128]{2,1,0:T(8,128)}, f32[8,64,128]{2,1,0:T(8,128)}, f32[8,64,128]{2,1,0:T(8,128)}) custom-call(f32[8,1024]{1,0:T(8,128)} %top.1, bf16[56,1024]{1,0:T(8,128)(2,1)} %one.1, bf16[448,1024]{1,0:T(8,128)(2,1)} %bitcast.5, bf16[56,64,1024]{2,1,0:T(8,128)(2,1)} %three_ref.1, ...), custom_call_target="tpu_custom_call" | custom-call | tf_op jit(solution)/shard_map/expand/pallas_call | solution.py:280
  9.6 6.2 %all-to-all-start = ((f32[32,64,128]{2,1,0:T(8,128)}), f32[32,64,128]{2,1,0:T(8,128)S(1)}, u32[]{:S(2)}, u32[]{:S(2)}) async-start(f32[32,64,128]{2,1,0:T(8,128)} %bitcast.4), calls=%async_computation | async-start | bytes 2097152 | tf_op jit(solution)/shard_map/all_to_all | solution.py:511
  15.8 1.3 collective-permute-start
  17.1 1.2 collective-permute-start.1
  18.3 0.2 collective-permute-start.2
  18.5 13.7 %collective-permute-done.refs_1_ = f32[8,64,128]{2,1,0:T(8,128)S(1)} collective-permute-done((f32[8,64,128]{2,1,0:T(8,128)S(1)}, f32[8,64,128]{2,1,0:T(8,128)S(1)}, u32[]{:S(2)}, u32[]{:S(2)}) %collective-permute-start) | collective-permute-done | bytes 262176 | tf_op jit(solution)/shard_map/ppermute | solution.py:434
  32.2 9.3 %collective-permute-done.2.refs_3_ = f32[8,64,128]{2,1,0:T(8,128)S(1)} collective-permute-done((f32[8,64,128]{2,1,0:T(8,128)S(1)}, f32[8,64,128]{2,1,0:T(8,128)S(1)}, u32[]{:S(2)}, u32[]{:S(2)}) %collective-permute-start.2) | collective-permute-done | bytes 262176 | tf_op jit(solution)/shard_map/ppermute | solution.py:434
  41.6 0.7 copy-done.3
  42.3 2.2 %regroup.1 = (f32[4,64,128]{2,1,0:T(8,128)}, f32[4,64,128]{2,1,0:T(8,128)}, f32[4,64,128]{2,1,0:T(8,128)}, f32[4,64,128]{2,1,0:T(8,128)}, f32[4,64,128]{2,1,0:T(...) custom-call(f32[8,64,128]{2,1,0:T(8,128)} %get-tuple-element.34.refs_0_, ...), custom_call_target="tpu_custom_call" | custom-call | tf_op jit(solution)/shard_map/regroup/pallas_call | solution.py:422
  44.5 0.8 collective-permute-start.3
  45.3 1.2 collective-permute-start.4
  46.5 0.5 collective-permute-start.5
  47.0 2.7 %collective-permute-start.7 = (f32[4,64,128]{2,1,0:T(8,128)}, f32[4,64,128]{2,1,0:T(8,128)S(1)}, u32[]{:S(2)}, u32[]{:S(2)}) collective-permute-start(f32[4,64,128]{2,1,0:T(8,128)} %get-tuple-element.43), channel_id=1, source_target_pairs={{0,5},{1,4},{2,7},{3,6},{4,1},{5,0},{6,3},{7,2},{8,13},{9,12},{10,... | collective-permute-start | bytes 393224 | tf_op jit(solution)/shard_map/ppermute | solution.py:434
  49.7 0.4 collective-permute-start.8
  50.1 0.5 collective-permute-done.4.refs_2_
  50.6 3.9 %collective-permute-start.9 = (f32[4,64,128]{2,1,0:T(8,128)}, f32[4,64,128]{2,1,0:T(8,128)S(1)}, u32[]{:S(2)}, u32[]{:S(2)}) collective-permute-start(f32[4,64,128]{2,1,0:T(8,128)} %get-tuple-element.45), channel_id=1, source_target_pairs={{0,7},{1,6},{2,5},{3,4},{4,3},{5,2},{6,1},{7,0},{8,15},{9,14},{10,... | collective-permute-start | bytes 393224 | tf_op jit(solution)/shard_map/ppermute | solution.py:434
  54.5 0.1 cosine_bitcast_fusion
  54.6 0.6 concatenate.3.refs_9_.refs_2_
  55.1 0.5 collective-permute-done.5.refs_3_
  55.7 0.7 collective-permute-done.6.refs_4_
  56.3 3.5 %collective-permute-done.7.refs_5_ = f32[4,64,128]{2,1,0:T(8,128)S(1)} collective-permute-done((f32[4,64,128]{2,1,0:T(8,128)}, f32[4,64,128]{2,1,0:T(8,128)S(1)}, u32[]{:S(2)}, u32[]{:S(2)}) %collective-permute-start.7) | collective-permute-done | bytes 131104 | tf_op jit(solution)/shard_map/ppermute | solution.py:434
  59.9 10.0 %collective-permute-done.8.refs_6_ = f32[4,64,128]{2,1,0:T(8,128)S(1)} collective-permute-done((f32[4,64,128]{2,1,0:T(8,128)}, f32[4,64,128]{2,1,0:T(8,128)S(1)}, u32[]{:S(2)}, u32[]{:S(2)}) %collective-permute-start.8) | collective-permute-done | bytes 131104 | tf_op jit(solution)/shard_map/ppermute | solution.py:434
  69.9 3.2 %collective-permute-done.9.refs_7_ = f32[4,64,128]{2,1,0:T(8,128)S(1)} collective-permute-done((f32[4,64,128]{2,1,0:T(8,128)}, f32[4,64,128]{2,1,0:T(8,128)S(1)}, u32[]{:S(2)}, u32[]{:S(2)}) %collective-permute-start.9) | collective-permute-done | bytes 131104 | tf_op jit(solution)/shard_map/ppermute | solution.py:434
  73.1 0.6 copy-done.20
  73.7 7.7 %middle.2 = (f32[2,128,128]{2,1,0:T(8,128)}, f32[2,128,128]{2,1,0:T(8,128)}, f32[2,128,128]{2,1,0:T(8,128)}, f32[2,128,128]{2,1,0:T(8,128)}, f32[2,128,128]{2,1,...) custom-call(f32[4,64,128]{2,1,0:T(8,128)} %get-tuple-element.38.refs_0_, ...), custom_call_target="tpu_custom_call" | custom-call | tf_op jit(solution)/shard_map/middle/pallas_call | solution.py:401
  81.4 0.0 collective-permute-start.10
  81.5 0.1 collective-permute-start.11
  81.6 1.0 copy-done
  82.5 7.5 %middle.3 = (f32[2,128,128]{2,1,0:T(8,128)}, f32[2,128,128]{2,1,0:T(8,128)}, f32[2,128,128]{2,1,0:T(8,128)}, f32[2,128,128]{2,1,0:T(8,128)}, f32[2,128,128]{2,1,...) custom-call(f32[32,64,128]{2,1,0:T(8,128)} %copy-done, f32[1024,128]{1,0:T(8,128)} %refs_1_.1, ...), custom_call_target="tpu_custom_call" | custom-call | tf_op jit(solution)/shard_map/middle/pallas_call | solution.py:401
  90.0 0.5 collective-permute-start.17
  90.5 1.7 %collective-permute-start.18 = (f32[2,128,128]{2,1,0:T(8,128)}, f32[2,128,128]{2,1,0:T(8,128)S(1)}, u32[]{:S(2)}, u32[]{:S(2)}) collective-permute-start(f32[2,128,128]{2,1,0:T(8,128)} %get-tuple-element.57), channel_id=1, source_target_pairs={{0,2},{1,3},{2,0},{3,1},{4,6},{5,7},{6,4},{7,5},{8,10},{9,11},{10,... | collective-permute-start | bytes 393224 | tf_op jit(solution)/shard_map/ppermute | solution.py:434
  92.3 1.1 collective-permute-start.20
  93.4 1.8 %collective-permute-start.21 = (f32[2,128,128]{2,1,0:T(8,128)}, f32[2,128,128]{2,1,0:T(8,128)S(1)}, u32[]{:S(2)}, u32[]{:S(2)}) collective-permute-start(f32[2,128,128]{2,1,0:T(8,128)} %get-tuple-element.60), channel_id=1, source_target_pairs={{0,5},{1,4},{2,7},{3,6},{4,1},{5,0},{6,3},{7,2},{8,13},{9,12},{10,... | collective-permute-start | bytes 393224 | tf_op jit(solution)/shard_map/ppermute | solution.py:434
  95.2 0.1 collective-permute-start.22
  95.3 1.0 collective-permute-done.18.refs_2_
  96.2 4.3 %collective-permute-start.23 = (f32[2,128,128]{2,1,0:T(8,128)}, f32[2,128,128]{2,1,0:T(8,128)S(1)}, u32[]{:S(2)}, u32[]{:S(2)}) collective-permute-start(f32[2,128,128]{2,1,0:T(8,128)} %get-tuple-element.62), channel_id=1, source_target_pairs={{0,7},{1,6},{2,5},{3,4},{4,3},{5,2},{6,1},{7,0},{8,15},{9,14},{10,... | collective-permute-start | bytes 393224 | tf_op jit(solution)/shard_map/ppermute | solution.py:434
  100.5 2.1 %collective-permute-start.12 = (f32[2,128,128]{2,1,0:T(8,128)S(1)}, f32[2,128,128]{2,1,0:T(8,128)S(1)}, u32[]{:S(2)}, u32[]{:S(2)}) collective-permute-start(f32[2,128,128]{2,1,0:T(8,128)S(1)} %copy-done.33), channel_id=1, source_target_pairs={{0,3},{1,2},{2,1},{3,0},{4,7},{5,6},{6,5},{7,4},{8,11},{9,10},{10,... | collective-permute-start | bytes 393224 | tf_op jit(solution)/shard_map/ppermute | solution.py:434
  102.6 1.8 %collective-permute-start.13 = (f32[2,128,128]{2,1,0:T(8,128)S(1)}, f32[2,128,128]{2,1,0:T(8,128)S(1)}, u32[]{:S(2)}, u32[]{:S(2)}) collective-permute-start(f32[2,128,128]{2,1,0:T(8,128)S(1)} %copy-done.32), channel_id=1, source_target_pairs={{0,4},{1,5},{2,6},{3,7},{4,0},{5,1},{6,2},{7,3},{8,12},{9,13},{10,... | collective-permute-start | bytes 393224 | tf_op jit(solution)/shard_map/ppermute | solution.py:434
  104.4 6.1 %collective-permute-done.21.refs_5_ = f32[2,128,128]{2,1,0:T(8,128)S(1)} collective-permute-done((f32[2,128,128]{2,1,0:T(8,128)}, f32[2,128,128]{2,1,0:T(8,128)S(1)}, u32[]{:S(2)}, u32[]{:S(2)}) %collective-permute-start.21) | collective-permute-done | bytes 131104 | tf_op jit(solution)/shard_map/ppermute | solution.py:434
  110.5 3.5 %collective-permute-start.14 = (f32[2,128,128]{2,1,0:T(8,128)S(1)}, f32[2,128,128]{2,1,0:T(8,128)S(1)}, u32[]{:S(2)}, u32[]{:S(2)}) collective-permute-start(f32[2,128,128]{2,1,0:T(8,128)S(1)} %copy-done.31), channel_id=1, source_target_pairs={{0,5},{1,4},{2,7},{3,6},{4,1},{5,0},{6,3},{7,2},{8,13},{9,12},{10,... | collective-permute-start | bytes 393224 | tf_op jit(solution)/shard_map/ppermute | solution.py:434
  114.0 7.3 %collective-permute-done.22.refs_6_ = f32[2,128,128]{2,1,0:T(8,128)S(1)} collective-permute-done((f32[2,128,128]{2,1,0:T(8,128)}, f32[2,128,128]{2,1,0:T(8,128)S(1)}, u32[]{:S(2)}, u32[]{:S(2)}) %collective-permute-start.22) | collective-permute-done | bytes 131104 | tf_op jit(solution)/shard_map/ppermute | solution.py:434
  121.3 9.4 %collective-permute-done.23.refs_7_ = f32[2,128,128]{2,1,0:T(8,128)S(1)} collective-permute-done((f32[2,128,128]{2,1,0:T(8,128)}, f32[2,128,128]{2,1,0:T(8,128)S(1)}, u32[]{:S(2)}, u32[]{:S(2)}) %collective-permute-start.23) | collective-permute-done | bytes 131104 | tf_op jit(solution)/shard_map/ppermute | solution.py:434
  130.8 0.6 copy-done.22
  131.3 2.2 %final.2.refs_8_ = f32[4,128,1024]{2,1,0:T(8,128)} custom-call(f32[2,128,128]{2,1,0:T(8,128)} %get-tuple-element.55.refs_0_, f32[2,128,128]{2,1,0:T(8,128)} %copy-done.8, f32[2,128,128]{2,1,0:T(8,128)} %copy-done.9, f32[2,128,128]{2,1,0:T(8,128)} %copy-done.10, f32[2,128,128]{2,1,0:T(8,128)} %copy-done.13, f32[2,128,128]{2,1,0:T(8,128)} %copy-done.16, ...), custom_call_target="tpu_custom_call" | custom-call | tf_op jit(solution)/shard_map/final/pallas_call | solution.py:477
  133.6 4.6 %collective-permute-done.15.refs_6_ = f32[2,128,128]{2,1,0:T(8,128)S(1)} collective-permute-done((f32[2,128,128]{2,1,0:T(8,128)S(1)}, f32[2,128,128]{2,1,0:T(8,128)S(1)}, u32[]{:S(2)}, u32[]{:S(2)}) %collective-permute-start.15) | collective-permute-done | bytes 131104 | tf_op jit(solution)/shard_map/ppermute | solution.py:434
  138.1 3.1 %collective-permute-done.16.refs_7_ = f32[2,128,128]{2,1,0:T(8,128)S(1)} collective-permute-done((f32[2,128,128]{2,1,0:T(8,128)S(1)}, f32[2,128,128]{2,1,0:T(8,128)S(1)}, u32[]{:S(2)}, u32[]{:S(2)}) %collective-permute-start.16) | collective-permute-done | bytes 131104 | tf_op jit(solution)/shard_map/ppermute | solution.py:434
  141.3 0.6 copy-done.24
  141.9 2.2 %final.3 = f32[4,128,1024]{2,1,0:T(8,128)} custom-call(f32[2,128,128]{2,1,0:T(8,128)} %get-tuple-element.46.refs_0_, f32[2,128,128]{2,1,0:T(8,128)} %copy-done.4, f32[2,128,128]{2,1,0:T(8,128)} %copy-done.5, f32[2,128,128]{2,1,0:T(8,128)} %copy-done.15, f32[2,128,128]{2,1,0:T(8,128)} %copy-done.18, ...), custom_call_target="tpu_custom_call", output_to_operand_aliasing={{}: (8, {})} | custom-call | tf_op jit(solution)/shard_map/final/pallas_call | solution.py:477
  (82 shorter events, 0.2 us)
Async XLA Ops:
  9.5 8.7 %copy-start.26 = (f32[8,64,128]{2,1,0:T(8,128)S(1)}, f32[8,64,128]{2,1,0:T(8,128)}, u32[]{:S(2)}) copy-start(f32[8,64,128]{2,1,0:T(8,128)} %get-tuple-element.37) | copy-start | bytes 786436
  9.5 44.9 %copy-start.25 = (s32[3,128]{1,0:T(4,128)S(1)}, s32[3,128]{1,0:T(4,128)}, u32[]{:S(2)}) copy-start(s32[3,128]{1,0:T(4,128)} %constant.38.clone) | copy-start | bytes 4612
  9.6 72.0 %all-to-all-start = ((f32[32,64,128]{2,1,0:T(8,128)}), f32[32,64,128]{2,1,0:T(8,128)S(1)}, u32[]{:S(2)}, u32[]{:S(2)}) async-start(f32[32,64,128]{2,1,0:T(8,128)} %bitcast.4), calls=%async_computation | async-start | bytes 2097152 | tf_op jit(solution)/shard_map/all_to_all | solution.py:511
  15.8 16.4 %collective-permute-start = (f32[8,64,128]{2,1,0:T(8,128)S(1)}, f32[8,64,128]{2,1,0:T(8,128)S(1)}, u32[]{:S(2)}, u32[]{:S(2)}) collective-permute-start(f32[8,64,128]{2,1,0:T(8,128)S(1)} %copy-done.28), channel_id=1, source_target_pairs={{0,8},{8,0},{16,24},{24,16},{1,9},{9,1},{17,25},{25,17},{2,10},{10... | collective-permute-start | bytes 786440 | tf_op jit(solution)/shard_map/ppermute | solution.py:434
  17.1 15.2 %collective-permute-start.1 = (f32[8,64,128]{2,1,0:T(8,128)S(1)}, f32[8,64,128]{2,1,0:T(8,128)S(1)}, u32[]{:S(2)}, u32[]{:S(2)}) collective-permute-start(f32[8,64,128]{2,1,0:T(8,128)S(1)} %copy-done.27), channel_id=1, source_target_pairs={{0,16},{8,24},{16,0},{24,8},{1,17},{9,25},{17,1},{25,9},{2,18},{10... | collective-permute-start | bytes 786440 | tf_op jit(solution)/shard_map/ppermute | solution.py:434
  18.3 23.3 %collective-permute-start.2 = (f32[8,64,128]{2,1,0:T(8,128)S(1)}, f32[8,64,128]{2,1,0:T(8,128)S(1)}, u32[]{:S(2)}, u32[]{:S(2)}) collective-permute-start(f32[8,64,128]{2,1,0:T(8,128)S(1)} %copy-done.26), channel_id=1, source_target_pairs={{0,24},{8,16},{16,8},{24,0},{1,25},{9,17},{17,9},{25,1},{2,26},{10... | collective-permute-start | bytes 786440 | tf_op jit(solution)/shard_map/ppermute | solution.py:434
  32.2 9.3 %copy-start.1 = (f32[8,64,128]{2,1,0:T(8,128)}, f32[8,64,128]{2,1,0:T(8,128)S(1)}, u32[]{:S(2)}) copy-start(f32[8,64,128]{2,1,0:T(8,128)S(1)} %collective-permute-done.refs_1_) | copy-start | bytes 786436
  32.2 9.3 %copy-start.2 = (f32[8,64,128]{2,1,0:T(8,128)}, f32[8,64,128]{2,1,0:T(8,128)S(1)}, u32[]{:S(2)}) copy-start(f32[8,64,128]{2,1,0:T(8,128)S(1)} %collective-permute-done.1.refs_2_) | copy-start | bytes 786436
  44.5 5.2 %collective-permute-start.3 = (f32[4,64,128]{2,1,0:T(8,128)}, f32[4,64,128]{2,1,0:T(8,128)S(1)}, u32[]{:S(2)}, u32[]{:S(2)}) collective-permute-start(f32[4,64,128]{2,1,0:T(8,128)} %get-tuple-element.39), channel_id=1, source_target_pairs={{0,1},{1,0},{2,3},{3,2},{4,5},{5,4},{6,7},{7,6},{8,9},{9,8},{10,11... | collective-permute-start | bytes 393224 | tf_op jit(solution)/shard_map/ppermute | solution.py:434
  45.3 5.2 %collective-permute-start.4 = (f32[4,64,128]{2,1,0:T(8,128)}, f32[4,64,128]{2,1,0:T(8,128)S(1)}, u32[]{:S(2)}, u32[]{:S(2)}) collective-permute-start(f32[4,64,128]{2,1,0:T(8,128)} %get-tuple-element.40), channel_id=1, source_target_pairs={{0,2},{1,3},{2,0},{3,1},{4,6},{5,7},{6,4},{7,5},{8,10},{9,11},{10,... | collective-permute-start | bytes 393224 | tf_op jit(solution)/shard_map/ppermute | solution.py:434
  46.5 9.1 %collective-permute-start.5 = (f32[4,64,128]{2,1,0:T(8,128)}, f32[4,64,128]{2,1,0:T(8,128)S(1)}, u32[]{:S(2)}, u32[]{:S(2)}) collective-permute-start(f32[4,64,128]{2,1,0:T(8,128)} %get-tuple-element.41), channel_id=1, source_target_pairs={{0,3},{1,2},{2,1},{3,0},{4,7},{5,6},{6,5},{7,4},{8,11},{9,10},{10,... | collective-permute-start | bytes 393224 | tf_op jit(solution)/shard_map/ppermute | solution.py:434
  47.0 9.3 %collective-permute-start.6 = (f32[4,64,128]{2,1,0:T(8,128)}, f32[4,64,128]{2,1,0:T(8,128)S(1)}, u32[]{:S(2)}, u32[]{:S(2)}) collective-permute-start(f32[4,64,128]{2,1,0:T(8,128)} %get-tuple-element.42), channel_id=1, source_target_pairs={{0,4},{1,5},{2,6},{3,7},{4,0},{5,1},{6,2},{7,3},{8,12},{9,13},{10,... | collective-permute-start | bytes 393224 | tf_op jit(solution)/shard_map/ppermute | solution.py:434
  47.0 12.9 %collective-permute-start.7 = (f32[4,64,128]{2,1,0:T(8,128)}, f32[4,64,128]{2,1,0:T(8,128)S(1)}, u32[]{:S(2)}, u32[]{:S(2)}) collective-permute-start(f32[4,64,128]{2,1,0:T(8,128)} %get-tuple-element.43), channel_id=1, source_target_pairs={{0,5},{1,4},{2,7},{3,6},{4,1},{5,0},{6,3},{7,2},{8,13},{9,12},{10,... | collective-permute-start | bytes 393224 | tf_op jit(solution)/shard_map/ppermute | solution.py:434
  49.7 23.3 %copy-start.6 = (f32[4,64,128]{2,1,0:T(8,128)}, f32[4,64,128]{2,1,0:T(8,128)S(1)}, u32[]{:S(2)}) copy-start(f32[4,64,128]{2,1,0:T(8,128)S(1)} %collective-permute-done.3.refs_1_) | copy-start | bytes 393220
  49.7 20.1 %collective-permute-start.8 = (f32[4,64,128]{2,1,0:T(8,128)}, f32[4,64,128]{2,1,0:T(8,128)S(1)}, u32[]{:S(2)}, u32[]{:S(2)}) collective-permute-start(f32[4,64,128]{2,1,0:T(8,128)} %get-tuple-element.44), channel_id=1, source_target_pairs={{0,6},{1,7},{2,4},{3,5},{4,2},{5,3},{6,0},{7,1},{8,14},{9,15},{10,... | collective-permute-start | bytes 393224 | tf_op jit(solution)/shard_map/ppermute | solution.py:434
  50.6 22.5 %copy-start.7 = (f32[4,64,128]{2,1,0:T(8,128)}, f32[4,64,128]{2,1,0:T(8,128)S(1)}, u32[]{:S(2)}) copy-start(f32[4,64,128]{2,1,0:T(8,128)S(1)} %collective-permute-done.4.refs_2_) | copy-start | bytes 393220
  50.6 22.5 %collective-permute-start.9 = (f32[4,64,128]{2,1,0:T(8,128)}, f32[4,64,128]{2,1,0:T(8,128)S(1)}, u32[]{:S(2)}, u32[]{:S(2)}) collective-permute-start(f32[4,64,128]{2,1,0:T(8,128)} %get-tuple-element.45), channel_id=1, source_target_pairs={{0,7},{1,6},{2,5},{3,4},{4,3},{5,2},{6,1},{7,0},{8,15},{9,14},{10,... | collective-permute-start | bytes 393224 | tf_op jit(solution)/shard_map/ppermute | solution.py:434
  55.7 17.4 %copy-start.11 = (f32[4,64,128]{2,1,0:T(8,128)}, f32[4,64,128]{2,1,0:T(8,128)S(1)}, u32[]{:S(2)}) copy-start(f32[4,64,128]{2,1,0:T(8,128)S(1)} %collective-permute-done.5.refs_3_) | copy-start | bytes 393220
  56.3 16.7 %copy-start.12 = (f32[4,64,128]{2,1,0:T(8,128)}, f32[4,64,128]{2,1,0:T(8,128)S(1)}, u32[]{:S(2)}) copy-start(f32[4,64,128]{2,1,0:T(8,128)S(1)} %collective-permute-done.6.refs_4_) | copy-start | bytes 393220
  59.9 13.2 %copy-start.14 = (f32[4,64,128]{2,1,0:T(8,128)}, f32[4,64,128]{2,1,0:T(8,128)S(1)}, u32[]{:S(2)}) copy-start(f32[4,64,128]{2,1,0:T(8,128)S(1)} %collective-permute-done.7.refs_5_) | copy-start | bytes 393220
  81.4 10.9 %collective-permute-start.10 = (f32[2,128,128]{2,1,0:T(8,128)}, f32[2,128,128]{2,1,0:T(8,128)S(1)}, u32[]{:S(2)}, u32[]{:S(2)}) collective-permute-start(f32[2,128,128]{2,1,0:T(8,128)} %get-tuple-element.47), channel_id=1, source_target_pairs={{0,1},{1,0},{2,3},{3,2},{4,5},{5,4},{6,7},{7,6},{8,9},{9,8},{10,11... | collective-permute-start | bytes 393224 | tf_op jit(solution)/shard_map/ppermute | solution.py:434
  81.4 19.1 %copy-start.33 = (f32[2,128,128]{2,1,0:T(8,128)S(1)}, f32[2,128,128]{2,1,0:T(8,128)}, u32[]{:S(2)}) copy-start(f32[2,128,128]{2,1,0:T(8,128)} %get-tuple-element.49) | copy-start | bytes 393220
  81.4 21.2 %copy-start.32 = (f32[2,128,128]{2,1,0:T(8,128)S(1)}, f32[2,128,128]{2,1,0:T(8,128)}, u32[]{:S(2)}) copy-start(f32[2,128,128]{2,1,0:T(8,128)} %get-tuple-element.50) | copy-start | bytes 393220
  81.4 29.1 %copy-start.31 = (f32[2,128,128]{2,1,0:T(8,128)S(1)}, f32[2,128,128]{2,1,0:T(8,128)}, u32[]{:S(2)}) copy-start(f32[2,128,128]{2,1,0:T(8,128)} %get-tuple-element.51) | copy-start | bytes 393220
  81.4 39.9 %copy-start.30 = (f32[2,128,128]{2,1,0:T(8,128)S(1)}, f32[2,128,128]{2,1,0:T(8,128)}, u32[]{:S(2)}) copy-start(f32[2,128,128]{2,1,0:T(8,128)} %get-tuple-element.52) | copy-start | bytes 393220
  81.5 49.2 %copy-start.29 = (f32[2,128,128]{2,1,0:T(8,128)S(1)}, f32[2,128,128]{2,1,0:T(8,128)}, u32[]{:S(2)}) copy-start(f32[2,128,128]{2,1,0:T(8,128)} %get-tuple-element.53) | copy-start | bytes 393220
  81.5 11.9 %collective-permute-start.11 = (f32[2,128,128]{2,1,0:T(8,128)}, f32[2,128,128]{2,1,0:T(8,128)S(1)}, u32[]{:S(2)}, u32[]{:S(2)}) collective-permute-start(f32[2,128,128]{2,1,0:T(8,128)} %get-tuple-element.48), channel_id=1, source_target_pairs={{0,2},{1,3},{2,0},{3,1},{4,6},{5,7},{6,4},{7,5},{8,10},{9,11},{10,... | collective-permute-start | bytes 393224 | tf_op jit(solution)/shard_map/ppermute | solution.py:434
  90.0 5.2 %collective-permute-start.17 = (f32[2,128,128]{2,1,0:T(8,128)}, f32[2,128,128]{2,1,0:T(8,128)S(1)}, u32[]{:S(2)}, u32[]{:S(2)}) collective-permute-start(f32[2,128,128]{2,1,0:T(8,128)} %get-tuple-element.56), channel_id=1, source_target_pairs={{0,1},{1,0},{2,3},{3,2},{4,5},{5,4},{6,7},{7,6},{8,9},{9,8},{10,11... | collective-permute-start | bytes 393224 | tf_op jit(solution)/shard_map/ppermute | solution.py:434
  90.5 5.7 %collective-permute-start.18 = (f32[2,128,128]{2,1,0:T(8,128)}, f32[2,128,128]{2,1,0:T(8,128)S(1)}, u32[]{:S(2)}, u32[]{:S(2)}) collective-permute-start(f32[2,128,128]{2,1,0:T(8,128)} %get-tuple-element.57), channel_id=1, source_target_pairs={{0,2},{1,3},{2,0},{3,1},{4,6},{5,7},{6,4},{7,5},{8,10},{9,11},{10,... | collective-permute-start | bytes 393224 | tf_op jit(solution)/shard_map/ppermute | solution.py:434
  92.2 8.3 %collective-permute-start.19 = (f32[2,128,128]{2,1,0:T(8,128)}, f32[2,128,128]{2,1,0:T(8,128)S(1)}, u32[]{:S(2)}, u32[]{:S(2)}) collective-permute-start(f32[2,128,128]{2,1,0:T(8,128)} %get-tuple-element.58), channel_id=1, source_target_pairs={{0,3},{1,2},{2,1},{3,0},{4,7},{5,6},{6,5},{7,4},{8,11},{9,10},{10,... | collective-permute-start | bytes 393224 | tf_op jit(solution)/shard_map/ppermute | solution.py:434
  92.2 49.0 %copy-start.4 = (f32[2,128,128]{2,1,0:T(8,128)}, f32[2,128,128]{2,1,0:T(8,128)S(1)}, u32[]{:S(2)}) copy-start(f32[2,128,128]{2,1,0:T(8,128)S(1)} %collective-permute-done.10.refs_1_) | copy-start | bytes 393220
  92.3 10.4 %collective-permute-start.20 = (f32[2,128,128]{2,1,0:T(8,128)}, f32[2,128,128]{2,1,0:T(8,128)S(1)}, u32[]{:S(2)}, u32[]{:S(2)}) collective-permute-start(f32[2,128,128]{2,1,0:T(8,128)} %get-tuple-element.59), channel_id=1, source_target_pairs={{0,4},{1,5},{2,6},{3,7},{4,0},{5,1},{6,2},{7,3},{8,12},{9,13},{10,... | collective-permute-start | bytes 393224 | tf_op jit(solution)/shard_map/ppermute | solution.py:434
  93.4 47.9 %copy-start.5 = (f32[2,128,128]{2,1,0:T(8,128)}, f32[2,128,128]{2,1,0:T(8,128)S(1)}, u32[]{:S(2)}) copy-start(f32[2,128,128]{2,1,0:T(8,128)S(1)} %collective-permute-done.11.refs_2_) | copy-start | bytes 393220
  93.4 17.1 %collective-permute-start.21 = (f32[2,128,128]{2,1,0:T(8,128)}, f32[2,128,128]{2,1,0:T(8,128)S(1)}, u32[]{:S(2)}, u32[]{:S(2)}) collective-permute-start(f32[2,128,128]{2,1,0:T(8,128)} %get-tuple-element.60), channel_id=1, source_target_pairs={{0,5},{1,4},{2,7},{3,6},{4,1},{5,0},{6,3},{7,2},{8,13},{9,12},{10,... | collective-permute-start | bytes 393224 | tf_op jit(solution)/shard_map/ppermute | solution.py:434
  95.2 35.5 %copy-start.8 = (f32[2,128,128]{2,1,0:T(8,128)}, f32[2,128,128]{2,1,0:T(8,128)S(1)}, u32[]{:S(2)}) copy-start(f32[2,128,128]{2,1,0:T(8,128)S(1)} %collective-permute-done.17.refs_1_) | copy-start | bytes 393220
  95.2 26.1 %collective-permute-start.22 = (f32[2,128,128]{2,1,0:T(8,128)}, f32[2,128,128]{2,1,0:T(8,128)S(1)}, u32[]{:S(2)}, u32[]{:S(2)}) collective-permute-start(f32[2,128,128]{2,1,0:T(8,128)} %get-tuple-element.61), channel_id=1, source_target_pairs={{0,6},{1,7},{2,4},{3,5},{4,2},{5,3},{6,0},{7,1},{8,14},{9,15},{10,... | collective-permute-start | bytes 393224 | tf_op jit(solution)/shard_map/ppermute | solution.py:434
  96.2 34.5 %copy-start.9 = (f32[2,128,128]{2,1,0:T(8,128)}, f32[2,128,128]{2,1,0:T(8,128)S(1)}, u32[]{:S(2)}) copy-start(f32[2,128,128]{2,1,0:T(8,128)S(1)} %collective-permute-done.18.refs_2_) | copy-start | bytes 393220
  96.2 34.5 %collective-permute-start.23 = (f32[2,128,128]{2,1,0:T(8,128)}, f32[2,128,128]{2,1,0:T(8,128)S(1)}, u32[]{:S(2)}, u32[]{:S(2)}) collective-permute-start(f32[2,128,128]{2,1,0:T(8,128)} %get-tuple-element.62), channel_id=1, source_target_pairs={{0,7},{1,6},{2,5},{3,4},{4,3},{5,2},{6,1},{7,0},{8,15},{9,14},{10,... | collective-permute-start | bytes 393224 | tf_op jit(solution)/shard_map/ppermute | solution.py:434
  100.5 30.2 %copy-start.10 = (f32[2,128,128]{2,1,0:T(8,128)}, f32[2,128,128]{2,1,0:T(8,128)S(1)}, u32[]{:S(2)}) copy-start(f32[2,128,128]{2,1,0:T(8,128)S(1)} %collective-permute-done.19.refs_3_) | copy-start | bytes 393220
  100.5 33.0 %collective-permute-start.12 = (f32[2,128,128]{2,1,0:T(8,128)S(1)}, f32[2,128,128]{2,1,0:T(8,128)S(1)}, u32[]{:S(2)}, u32[]{:S(2)}) collective-permute-start(f32[2,128,128]{2,1,0:T(8,128)S(1)} %copy-done.33), channel_id=1, source_target_pairs={{0,3},{1,2},{2,1},{3,0},{4,7},{5,6},{6,5},{7,4},{8,11},{9,10},{10,... | collective-permute-start | bytes 393224 | tf_op jit(solution)/shard_map/ppermute | solution.py:434
  102.6 28.1 %copy-start.13 = (f32[2,128,128]{2,1,0:T(8,128)}, f32[2,128,128]{2,1,0:T(8,128)S(1)}, u32[]{:S(2)}) copy-start(f32[2,128,128]{2,1,0:T(8,128)S(1)} %collective-permute-done.20.refs_4_) | copy-start | bytes 393220
  102.6 30.9 %collective-permute-start.13 = (f32[2,128,128]{2,1,0:T(8,128)S(1)}, f32[2,128,128]{2,1,0:T(8,128)S(1)}, u32[]{:S(2)}, u32[]{:S(2)}) collective-permute-start(f32[2,128,128]{2,1,0:T(8,128)S(1)} %copy-done.32), channel_id=1, source_target_pairs={{0,4},{1,5},{2,6},{3,7},{4,0},{5,1},{6,2},{7,3},{8,12},{9,13},{10,... | collective-permute-start | bytes 393224 | tf_op jit(solution)/shard_map/ppermute | solution.py:434
  110.5 20.3 %copy-start.16 = (f32[2,128,128]{2,1,0:T(8,128)}, f32[2,128,128]{2,1,0:T(8,128)S(1)}, u32[]{:S(2)}) copy-start(f32[2,128,128]{2,1,0:T(8,128)S(1)} %collective-permute-done.21.refs_5_) | copy-start | bytes 393220
  110.5 23.1 %collective-permute-start.14 = (f32[2,128,128]{2,1,0:T(8,128)S(1)}, f32[2,128,128]{2,1,0:T(8,128)S(1)}, u32[]{:S(2)}, u32[]{:S(2)}) collective-permute-start(f32[2,128,128]{2,1,0:T(8,128)S(1)} %copy-done.31), channel_id=1, source_target_pairs={{0,5},{1,4},{2,7},{3,6},{4,1},{5,0},{6,3},{7,2},{8,13},{9,12},{10,... | collective-permute-start | bytes 393224 | tf_op jit(solution)/shard_map/ppermute | solution.py:434
  121.3 9.5 %copy-start.19 = (f32[2,128,128]{2,1,0:T(8,128)}, f32[2,128,128]{2,1,0:T(8,128)S(1)}, u32[]{:S(2)}) copy-start(f32[2,128,128]{2,1,0:T(8,128)S(1)} %collective-permute-done.22.refs_6_) | copy-start | bytes 393220
  121.3 16.8 %collective-permute-start.15 = (f32[2,128,128]{2,1,0:T(8,128)S(1)}, f32[2,128,128]{2,1,0:T(8,128)S(1)}, u32[]{:S(2)}, u32[]{:S(2)}) collective-permute-start(f32[2,128,128]{2,1,0:T(8,128)S(1)} %copy-done.30), channel_id=1, source_target_pairs={{0,6},{1,7},{2,4},{3,5},{4,2},{5,3},{6,0},{7,1},{8,14},{9,15},{10,... | collective-permute-start | bytes 393224 | tf_op jit(solution)/shard_map/ppermute | solution.py:434
  130.7 10.6 %collective-permute-start.16 = (f32[2,128,128]{2,1,0:T(8,128)S(1)}, f32[2,128,128]{2,1,0:T(8,128)S(1)}, u32[]{:S(2)}, u32[]{:S(2)}) collective-permute-start(f32[2,128,128]{2,1,0:T(8,128)S(1)} %copy-done.29), channel_id=1, source_target_pairs={{0,7},{1,6},{2,5},{3,4},{4,3},{5,2},{6,1},{7,0},{8,15},{9,14},{10,... | collective-permute-start | bytes 393224 | tf_op jit(solution)/shard_map/ppermute | solution.py:434
  133.5 7.8 %copy-start.15 = (f32[2,128,128]{2,1,0:T(8,128)}, f32[2,128,128]{2,1,0:T(8,128)S(1)}, u32[]{:S(2)}) copy-start(f32[2,128,128]{2,1,0:T(8,128)S(1)} %collective-permute-done.12.refs_3_) | copy-start | bytes 393220
  (11 other events, 39.3 us)
